TPU v7x, 256 devices: a whole 4x4x8 slice. The times are simulated.
256 devices in a mesh: seq: 32 (over x_hi, z, core), tensor: 8 (over x_lo, y).
Axes of the slice: x: 4 (x_hi: 2, x_lo: 2; x = x_hi * 2 + x_lo), y: 4, z: 8, core: 2. Of those that a mesh axis runs over, the one named last changes fastest.
Arguments:
- hidden: bfloat16 [8192, 2304], P('seq', 'tensor'), may hold values from -6 to 6
- attn_gain: float32 [2304], replicated, may hold values from 0.1 to 1.9
- query_weight: bfloat16 [2304, 2048], P(None, 'tensor'), may hold values from -1 to 1
- kv_weight: bfloat16 [2304, 2048], P(None, 'tensor'), may hold values from -1 to 1
- out_weight: bfloat16 [2048, 2304], P('tensor'), may hold values from -0.125 to 0.125
- post_gain: float32 [2304], replicated, may hold values from 0.1 to 1.9
- ff_gain: float32 [2304], replicated, may hold values from 0.1 to 1.9
- ff_post_gain: float32 [2304], replicated, may hold values from 0.1 to 1.9
- gate_weight: bfloat16 [2304, 9216], P('seq', 'tensor'), may hold values from -0.125 to 0.125
- up_weight: bfloat16 [2304, 9216], P('seq', 'tensor'), may hold values from -0.125 to 0.125
- down_weight_t: bfloat16 [2304, 9216], P('seq', 'tensor'), may hold values from -0.0625 to 0.0625
- next_gain: float32 [2304], replicated, may hold values from 0.1 to 1.9
- next_query_weight: bfloat16 [2304, 2048], P(None, 'tensor'), may hold values from -0.125 to 0.125
- next_kv_weight: bfloat16 [2304, 2048], P(None, 'tensor'), may hold values from -0.125 to 0.125
- lengths: int32 [4], replicated, may hold values from 256 to 3840, as said below
- pair_owner: int32 [32], replicated, may hold values from 0 to 31, each once
- page_table: int32 [64], replicated, may hold values from 0 to 63, each once
Outputs:
- hidden_out: bfloat16 [8192, 2304], P('seq', 'tensor')
- next_query: bfloat16 [8192, 2048], P('seq', 'tensor')
- next_kv: bfloat16 [8192, 2048], P('seq', 'tensor')
- kv_pages: bfloat16 [64, 128, 2048], P('seq', None, 'tensor')
Inputs may be any that keep to these rules, and one draw needn't show every extreme that they name: Four positive lengths summing to 8192; the first is the longest and the fourth the shortest. `pair_owner`: each mirrored pair b, the blocks b and 63 - b, is held by exactly one index of seq. `page_table`: every page takes exactly one block.
All inputs are finite; a program needn't handle non-finite values.
Results may differ from a plain program's by a relative error of at most 0.018.
Values may be sent and summed in bfloat16 or wider, within the bound.
A program may use at most 128 MiB of HBM per device.

v0:
```python
import jax
import jax.numpy as jnp
from jax import lax
from jax.sharding import PartitionSpec as P

EPS = 1e-06
SOFT_CAP = 50.0


def partner_2(block, axis, apart):
    count = lax.axis_size(axis)
    route = []
    for low in range(count):
        high = low | 1 << apart
        if high != low and high < count:
            route += [(low, high), (high, low)]
    return lax.ppermute(block, axis, route)


def row_norm(values, gain_vec):
    values = values.astype(jnp.float32)
    scale_vec = lax.rsqrt(jnp.mean(values * values, axis=-1, keepdims=True) + EPS)
    return values * scale_vec * gain_vec


def rotate(values, positions):
    half_dim = values.shape[-1] // 2
    freq_vec = 10000.0 ** (-jnp.arange(half_dim, dtype=jnp.float32) / half_dim)
    angles = positions.astype(jnp.float32)[:, None] * freq_vec[None, :]
    cosine_val = jnp.cos(angles)
    sine_val = jnp.sin(angles)
    leading = values[:, :half_dim]
    trailing = values[:, half_dim:]
    return jnp.concatenate(
        [leading * cosine_val - trailing * sine_val, trailing * cosine_val + leading * sine_val],
        axis=1,
    )


def tenant_of(stream_index, lengths):
    tenant_ends = jnp.cumsum(lengths)
    tenant_starts = tenant_ends - lengths
    tenant = jnp.sum((stream_index[:, None] >= tenant_ends[None, :3]).astype(jnp.int32), axis=1)
    selector = tenant[:, None] == jnp.arange(4, dtype=jnp.int32)[None, :]
    offset = jnp.sum(jnp.where(selector, tenant_starts[None, :], 0), axis=1)
    return (tenant, (stream_index - offset).astype(jnp.int32))


def body(
    hidden,
    attn_gain,
    query_weight,
    kv_weight,
    out_weight,
    post_gain,
    ff_gain,
    ff_post_gain,
    gate_weight,
    up_weight,
    down_weight_t,
    next_gain,
    next_query_weight,
    next_kv_weight,
    lengths,
    pair_owner,
    page_table,
):
    seq_count = lax.axis_size("seq")
    seq_index = lax.axis_index("seq")
    tensor_index = lax.axis_index("tensor")
    rows = hidden.shape[0]
    rows_half = rows // 2
    share = hidden.shape[1]
    head_dim = query_weight.shape[1]
    is_key = tensor_index % 2 == 0
    owned_pair = jnp.sum(
        jnp.where(jnp.arange(seq_count, dtype=jnp.int32) == seq_index, pair_owner, 0)
    )
    local_range = jnp.arange(rows_half, dtype=jnp.int32)
    tags = jnp.concatenate(
        [
            owned_pair * rows_half + local_range,
            (2 * seq_count - 1 - owned_pair) * rows_half + local_range,
        ]
    )
    tenant, position = tenant_of(tags, lengths)
    block_ids = jnp.arange(2 * seq_count, dtype=jnp.int32)
    page_blocks = [
        jnp.sum(jnp.where(page_table == 2 * seq_index + slot_index, block_ids, 0))
        for slot_index in range(2)
    ]
    wanted_tags = jnp.concatenate(
        [page_blocks[0] * rows_half + local_range, page_blocks[1] * rows_half + local_range]
    )
    full_hidden = lax.all_gather(hidden, "tensor", axis=1, tiled=True)
    attn_input = row_norm(full_hidden, attn_gain).astype(jnp.bfloat16)
    queries = rotate(
        jnp.dot(attn_input, query_weight, preferred_element_type=jnp.float32), position
    ).astype(jnp.bfloat16)
    own_proj = jnp.dot(attn_input, kv_weight, preferred_element_type=jnp.float32)
    own_part = jnp.where(is_key, rotate(own_proj, position), own_proj).astype(jnp.bfloat16)
    query_scale = head_dim ** (-0.5)
    partner = partner_2(own_part, "tensor", 0)
    key_mine = jnp.where(is_key, own_part, partner)
    value_mine = jnp.where(is_key, partner, own_part)
    key_rows = lax.all_gather(key_mine, "seq", axis=0, tiled=True)
    value_rows = lax.all_gather(value_mine, "seq", axis=0, tiled=True)
    key_tags = lax.all_gather(tags, "seq", axis=0, tiled=True)
    key_tenant, key_position = tenant_of(key_tags, lengths)
    allowed = (tenant[:, None] == key_tenant[None, :]) & (key_tags[None, :] <= tags[:, None])
    raw_scores = (
        lax.dot_general(
            queries, key_rows, (((1,), (1,)), ((), ())), preferred_element_type=jnp.float32
        )
        * query_scale
    )
    capped = SOFT_CAP * jnp.tanh(raw_scores / SOFT_CAP)
    weights = jnp.where(allowed, jnp.exp(capped), 0.0).astype(jnp.bfloat16)
    own_rows = jnp.where(is_key, key_rows, value_rows)
    numerator = jnp.dot(weights, value_rows, preferred_element_type=jnp.float32)
    denominator = jnp.sum(weights.astype(jnp.float32), axis=1)
    picker = (wanted_tags[:, None] == key_tags[None, :]).astype(jnp.bfloat16)
    cache_acc = jnp.dot(picker, own_rows, preferred_element_type=jnp.float32)
    attended = (numerator / denominator[:, None]).astype(jnp.bfloat16)
    attn_partial = jnp.dot(attended, out_weight, preferred_element_type=jnp.float32)
    column_start = tensor_index * share
    attn_sum = lax.psum(attn_partial, "tensor")
    middle = (full_hidden.astype(jnp.float32) + row_norm(attn_sum, post_gain)).astype(jnp.bfloat16)
    ff_input = row_norm(middle, ff_gain).astype(jnp.bfloat16)
    gate_val = jnp.dot(
        ff_input,
        lax.all_gather(gate_weight, "seq", axis=0, tiled=True),
        preferred_element_type=jnp.float32,
    )
    up_val = jnp.dot(
        ff_input,
        lax.all_gather(up_weight, "seq", axis=0, tiled=True),
        preferred_element_type=jnp.float32,
    )
    inner = (jax.nn.gelu(gate_val, approximate=True) * up_val).astype(jnp.bfloat16)
    ff_partial = lax.dot_general(
        inner,
        lax.all_gather(down_weight_t, "seq", axis=0, tiled=True),
        (((1,), (1,)), ((), ())),
        preferred_element_type=jnp.float32,
    )
    ff_sum = lax.psum(ff_partial.astype(jnp.bfloat16), "tensor").astype(jnp.float32)
    final_rows = (middle.astype(jnp.float32) + row_norm(ff_sum, ff_post_gain)).astype(jnp.bfloat16)
    next_input = row_norm(final_rows, next_gain).astype(jnp.bfloat16)
    hidden_out = lax.dynamic_slice_in_dim(final_rows, column_start, share, 1)
    next_query = rotate(
        jnp.dot(next_input, next_query_weight, preferred_element_type=jnp.float32), position
    ).astype(jnp.bfloat16)
    next_proj = jnp.dot(next_input, next_kv_weight, preferred_element_type=jnp.float32)
    next_kv = jnp.where(is_key, rotate(next_proj, position), next_proj).astype(jnp.bfloat16)
    kv_pages = cache_acc.astype(jnp.bfloat16).reshape(2, rows_half, head_dim)
    return (hidden_out, next_query, next_kv, kv_pages)


def solution(mesh):
    in_specs = (
        P("seq", "tensor"),
        P(),
        P(None, "tensor"),
        P(None, "tensor"),
        P("tensor", None),
        P(),
        P(),
        P(),
        P("seq", "tensor"),
        P("seq", "tensor"),
        P("seq", "tensor"),
        P(),
        P(None, "tensor"),
        P(None, "tensor"),
        P(),
        P(),
        P(),
    )
    out_specs = (
        P("seq", "tensor"),
        P("seq", "tensor"),
        P("seq", "tensor"),
        P("seq", None, "tensor"),
    )
    return jax.shard_map(body, mesh=mesh, in_specs=in_specs, out_specs=out_specs, check_vma=False)
```

profile of v0, /device:TPU:4, one launch (start us, length us, event | category | flops | bytes accessed | tf_op | source)
XLA Modules:
  0.0 710.7 jit_solution(15065292437494655086)
XLA Ops:
  8.0 1.3 fusion.89
  10.6 0.8 reduce-window.4
  12.3 41.9 %all-gather.8.cloned.1.call-done = bf16[256,2304]{0,1:T(8,128)(2,1)} async-done(((bf16[256,288]{0,1:T(8,128)(2,1)}), bf16[256,2304]{0,1:T(8,128)(2,1)}) %all-gather.8.cloned.1.call-update) | async-done | bytes 1179664 | tf_op jit(solution)/shard_map/all_gather | solution.py:95
  54.2 1.6 copy.29
  56.1 2.0 fusion.47
  58.9 5.0 collective-permute-done
  65.4 40.0 %all-gather = s32[32,1,256]{2,1,0:T(1,128)S(1)} all-gather(s32[1,1,256]{2,1,0:T(1,128)S(1)} %bitcast.22), channel_id=1, replica_groups=mesh['seq'=32,'tensor'=8] {'seq'}, dimensions={0}, use_global_device_ids=true | all-gather | bytes 33792 | tf_op jit(solution)/shard_map/all_gather | solution.py:108
  105.5 2.0 fusion.49
  108.1 40.5 %all-gather.10.cloned.1.call-done = bf16[8192,256]{0,1:T(8,128)(2,1)} async-done(((bf16[256,256]{0,1:T(8,128)(2,1)}), bf16[8192,256]{0,1:T(8,128)(2,1)}) %all-gather.10.cloned.1.call-update) | async-done | bytes 4194320 | tf_op jit(solution)/shard_map/all_gather | solution.py:106
  148.7 7.5 %convert_reduce_fusion = (f32[256]{0:T(256)S(1)}, bf16[256,8192]{1,0:T(8,128)(2,1)}) fusion(bf16[8192,256]{0,1:T(8,128)(2,1)} %all-gather.10.cloned.1.call-done, bf16[256,128]{0,1:T(8,128)(2,1)S(1)} %get-tuple-element.27, bf16[256,128]{0,1:T(8,128)(2,1)S(1)} %get-tuple-element.26, s32[256]{0:T(256)S(1)} %pad_add_fusion, s32[8192]{0:T(1024)S(1)} %bitcast.20, ...), kind=kOutput, calls=%fused_computation.6 | convolution fusion | flops 1092878080 | bytes 8588288 | tf_op jit(solution)/shard_map/dot_general | solution.py:112
  156.1 79.5 %all-gather.12.cloned.1.call-done = bf16[8192,256]{0,1:T(8,128)(2,1)} async-done(((bf16[256,256]{0,1:T(8,128)(2,1)}), bf16[8192,256]{0,1:T(8,128)(2,1)}) %all-gather.12.cloned.1.call-update) | async-done | bytes 4194320 | tf_op jit(solution)/shard_map/all_gather | solution.py:107
  235.6 7.2 %fusion.38 = f32[256,2304]{1,0:T(8,128)} fusion(bf16[256,2304]{1,0:T(8,128)(2,1)S(1)} %copy-done, bf16[256,8192]{1,0:T(8,128)(2,1)} %get-tuple-element.33, bf16[8192,256]{0,1:T(8,128)(2,1)} %all-gather.12.cloned.1.call-done, f32[256]{0:T(256)S(1)} %get-tuple-element.32), kind=kOutput, calls=%fused_computation.51 | convolution fusion | flops 1375862784 | bytes 11928576 | tf_op jit(solution)/shard_map/dot_general | solution.py:125
  245.0 86.2 %all-reduce.3.cloned.1.call-done = f32[256,2304]{1,0:T(8,128)} async-done(((f32[256,2304]{1,0:T(8,128)}), f32[256,2304]{1,0:T(8,128)}) %all-reduce.3.cloned.1.call-update) | async-done | bytes 2359312 | tf_op jit(solution)/shard_map/psum | solution.py:127
  331.2 2.1 multiply_reduce_fusion
  334.3 88.3 %all-gather.14.cloned.1.call-done = bf16[2304,1152]{1,0:T(8,128)(2,1)} async-done(((bf16[72,1152]{1,0:T(8,128)(2,1)}), bf16[2304,1152]{1,0:T(8,128)(2,1)}) %all-gather.14.cloned.1.call-update) | async-done | bytes 5308432 | tf_op jit(solution)/shard_map/all_gather | solution.py:132
  422.6 5.4 fusion.45
  427.9 84.7 %all-gather.16.cloned.1.call-done = bf16[2304,1152]{1,0:T(8,128)(2,1)} async-done(((bf16[72,1152]{1,0:T(8,128)(2,1)}), bf16[2304,1152]{1,0:T(8,128)(2,1)}) %all-gather.16.cloned.1.call-update) | async-done | bytes 5308432 | tf_op jit(solution)/shard_map/all_gather | solution.py:137
  512.7 90.3 %all-gather.18.cloned.1.call-done = bf16[2304,1152]{1,0:T(8,128)(2,1)} async-done(((bf16[72,1152]{1,0:T(8,128)(2,1)}), bf16[2304,1152]{1,0:T(8,128)(2,1)}) %all-gather.18.cloned.1.call-update) | async-done | bytes 5308432 | tf_op jit(solution)/shard_map/all_gather | solution.py:143
  602.9 8.8 %convolution_convert_fusion = bf16[256,2304]{1,0:T(8,128)(2,1)} fusion(bf16[2304,1152]{1,0:T(8,128)(2,1)} %all-gather.18.cloned.1.call-done, bf16[2304,1152]{1,0:T(8,128)(2,1)} %all-gather.16.cloned.1.call-done, f32[256,1152]{1,0:T(8,128)} %fusion.45, bf16[256,2304]{1,0:T(8,128)(2,1)S(1)} %get-tuple-element.21, f32[2304]{0:T(1024)S(1)} %copy-done.11, ...), kind=kOutput, calls=%fused_computation.13 | convolution fusion | flops 2723807232 | bytes 14166016 | tf_op jit(solution)/shard_map/dot_general | solution.py:141
  613.8 4.4 fusion.32
  618.2 75.5 %all-reduce.5.cloned.1.call-done = bf16[256,2304]{1,0:T(8,128)(2,1)} async-done(((bf16[256,2304]{1,0:T(8,128)(2,1)}), bf16[256,2304]{1,0:T(8,128)(2,1)}) %all-reduce.5.cloned.1.call-update) | async-done | bytes 1179664 | tf_op jit(solution)/shard_map/psum | solution.py:147
  693.7 1.7 fusion.12
  695.4 2.0 fusion.14
  699.6 2.0 fusion.53
  (77 shorter events, 13.1 us)
Async XLA Ops:
  7.2 228.4 %copy-start = (bf16[256,2304]{1,0:T(8,128)(2,1)S(1)}, bf16[256,2304]{1,0:T(8,128)(2,1)}, u32[]{:S(2)}) copy-start(bf16[256,2304]{1,0:T(8,128)(2,1)} %param.21) | copy-start | bytes 3538948
  7.2 49.0 %copy-start.10 = (f32[2304]{0:T(1024)S(1)}, f32[2304]{0:T(1024)}, u32[]{:S(2)}) copy-start(f32[2304]{0:T(1024)} %param.18) | copy-start | bytes 27652
  7.2 47.0 %all-gather.8.cloned.1.call-start = ((), (), s32[]{:S(2)}) async-start(), calls=%async_computation | async-start | bytes 1327104 | tf_op jit(solution)/shard_map/all_gather | solution.py:95
  7.9 140.7 %all-gather.10.cloned.1.call-start = ((), (), s32[]{:S(2)}) async-start(), calls=%async_computation.1 | async-start | bytes 4325376 | tf_op jit(solution)/shard_map/all_gather | solution.py:106
  11.4 96.1 %copy-start.6 = (f32[128]{0:T(128)}, f32[128]{0:T(128)S(1)}, u32[]{:S(2)}) copy-start(f32[128]{0:T(128)S(1)} %multiply_power_fusion) | copy-start | bytes 1540
  58.8 5.1 collective-permute-start
  64.6 171.0 %all-gather.12.cloned.1.call-start = ((), (), s32[]{:S(2)}) async-start(), calls=%async_computation.2 | async-start | bytes 4325376 | tf_op jit(solution)/shard_map/all_gather | solution.py:107
  65.3 265.9 %all-reduce.3.cloned.1.call-start = ((), (), s32[]{:S(2)}) async-start(), calls=%async_computation.3 | async-start | bytes 4718592 | tf_op jit(solution)/shard_map/psum | solution.py:127
  105.4 50.8 %copy-start.2 = (s32[32,1,256]{2,1,0:T(1,128)}, s32[32,1,256]{2,1,0:T(1,128)S(1)}, u32[]{:S(2)}) copy-start(s32[32,1,256]{2,1,0:T(1,128)S(1)} %all-gather) | copy-start | bytes 98308
  242.8 90.4 %copy-start.4 = (f32[2304]{0:T(1024)S(1)}, f32[2304]{0:T(1024)}, u32[]{:S(2)}) copy-start(f32[2304]{0:T(1024)} %param.22) | copy-start | bytes 27652
  242.9 179.7 %all-gather.14.cloned.1.call-start = ((), (), s32[]{:S(2)}) async-start(), calls=%async_computation.4 | async-start | bytes 5474304 | tf_op jit(solution)/shard_map/all_gather | solution.py:132
  243.5 269.2 %all-gather.16.cloned.1.call-start = ((), (), s32[]{:S(2)}) async-start(), calls=%async_computation.5 | async-start | bytes 5474304 | tf_op jit(solution)/shard_map/all_gather | solution.py:137
  244.0 358.9 %all-gather.18.cloned.1.call-start = ((), (), s32[]{:S(2)}) async-start(), calls=%async_computation.6 | async-start | bytes 5474304 | tf_op jit(solution)/shard_map/all_gather | solution.py:143
  244.8 448.9 %all-reduce.5.cloned.1.call-start = ((), (), s32[]{:S(2)}) async-start(), calls=%async_computation.7 | async-start | bytes 2359296 | tf_op jit(solution)/shard_map/psum | solution.py:147
  331.2 2.4 copy-start.1
  422.6 180.4 %copy-start.11 = (f32[2304]{0:T(1024)S(1)}, f32[2304]{0:T(1024)}, u32[]{:S(2)}) copy-start(f32[2304]{0:T(1024)} %param.23) | copy-start | bytes 27652
  427.9 183.9 %copy-start.8 = (s32[64]{0:T(128)S(1)}, s32[64]{0:T(128)}, u32[]{:S(2)}) copy-start(s32[64]{0:T(128)} %param.33) | copy-start | bytes 772
  427.9 185.8 %copy-start.3 = (s32[32,1,256]{2,1,0:T(1,128)S(1)}, s32[32,1,256]{2,1,0:T(1,128)}, u32[]{:S(2)}) copy-start(s32[32,1,256]{2,1,0:T(1,128)} %copy-done.2) | copy-start | bytes 98308
  613.8 81.6 %copy-start.5 = (f32[2304]{0:T(1024)S(1)}, f32[2304]{0:T(1024)}, u32[]{:S(2)}) copy-start(f32[2304]{0:T(1024)} %param.24) | copy-start | bytes 27652
  693.7 3.7 copy-start.9
  693.7 3.7 copy-start.12
  697.4 0.8 copy-start.7
  697.4 2.2 copy-start.13
Sparse Core Ops, SparseCore 0:
  9.8 44.3 all-gather.7
  64.7 83.9 all-gather.9
  151.8 83.7 all-gather.11
  243.0 88.1 all-reduce.2
  333.7 88.7 all-gather.13
  425.1 87.5 all-gather.15
  515.4 87.5 all-gather.17
  611.9 81.7 all-reduce.4
where the time goes:
time: 711 us
  waiting for transfers between devices  595 us (84%)
  matrix products  40.1 us (6%)
  blocking collectives  40 us (6%)
  between operations  17 us (2%)
  other arithmetic  13.6 us (2%)
    all_gather x1, waiting for transfers between devices, body(): lax.all_gather(down_weight_t, 'seq', axis=0, tiled=True)  90.3 us
    all_gather x1, waiting for transfers between devices, body(): lax.all_gather(gate_weight, 'seq', axis=0, tiled=True)  88.3 us
    psum x1, waiting for transfers between devices, body(): attn_sum = lax.psum(attn_partial, 'tensor')  86.2 us
    all_gather x1, waiting for transfers between devices, body(): lax.all_gather(up_weight, 'seq', axis=0, tiled=True)  84.7 us
    all_gather x1, waiting for transfers between devices, body(): value_rows = lax.all_gather(value_mine, 'seq', axis=0, tiled=True)  79.5 us
    psum x1, waiting for transfers between devices, body(): lax.psum(ff_partial.astype(jnp.bfloat16), 'tensor').astype(jnp.float32)  75.5 us
    all_gather x1, waiting for transfers between devices, body(): full_hidden = lax.all_gather(hidden, 'tensor', axis=1, tiled=True)  41.9 us
    all_gather x1, waiting for transfers between devices, body(): key_rows = lax.all_gather(key_mine, 'seq', axis=0, tiled=True)  40.5 us
  transfers between devices with their start and end apart: 9, of which 9 were waited for; matrix products, arithmetic and copies ran while one was open for 4% of the time, Pallas kernels for 0%

commit v1 on v0

v1 whole, which is shorter than its diff:
```python
import functools

import jax
import jax.numpy as jnp
from jax import lax
from jax.experimental import pallas as pl
from jax.experimental.pallas import tpu as pltpu
from jax.sharding import PartitionSpec as P

EPS = 1e-06
SOFT_CAP = 50.0
MESH = pl.DeviceIdType.MESH
VM = pl.BlockSpec(memory_space=pltpu.VMEM)
AN = pl.BlockSpec(memory_space=pl.ANY)
FFP = 640
FFO = 512
bf16 = jnp.bfloat16
f32 = jnp.float32


class Place:
    def __init__(self):
        self.s = lax.axis_index("seq")
        self.t = lax.axis_index("tensor")
        self.x = self.s // 16
        self.z = (self.s // 2) % 8
        self.c = self.s % 2
        self.yb = self.t % 2

    def seq(self, x, z, c):
        return x * 16 + z * 2 + c

    def dev(self, s, t):
        return {"seq": s, "tensor": t}

    def zp(self):
        return self.dev(self.seq(self.x, (self.z + 1) % 8, self.c), self.t)

    def zm(self):
        return self.dev(self.seq(self.x, (self.z + 7) % 8, self.c), self.t)

    def sib(self):
        return self.dev(self.seq(self.x, self.z, 1 - self.c), self.t)

    def xpart(self):
        return self.dev(self.seq(1 - self.x, self.z, self.c), self.t)

    def quad(self, o):
        dx, dy = o // 2, o % 2
        x = (self.x + dx) % 2
        yb = (self.yb + dy) % 2
        return x, yb, self.dev(self.seq(x, self.z, self.c), self.t - self.yb + yb)

    def tens(self, o):
        t = (self.t + o) % 8
        return t, self.dev(self.s, t)

    def plane(self, o):
        j = (self.x * 8 + self.t + o) % 16
        x, t = j // 8, j % 8
        return j, self.dev(self.seq(x, self.z, self.c), t)


class Copies:
    def __init__(self, send, recv):
        self.send, self.recv, self.n, self.live = send, recv, 0, []

    def make(self, src, dst, dev):
        i = self.n
        self.n += 1
        return pltpu.make_async_remote_copy(
            src_ref=src, dst_ref=dst, send_sem=self.send.at[i], recv_sem=self.recv.at[i],
            device_id=dev, device_id_type=MESH,
        )

    def go(self, src, dst, dev):
        cp = self.make(src, dst, dev)
        cp.start()
        self.live.append(cp)
        return cp

    def drain_sends(self):
        for cp in self.live:
            cp.wait_send()


def barrier(peers):
    sem = pltpu.get_barrier_semaphore()
    for dev in peers:
        pl.semaphore_signal(sem, inc=1, device_id=dev, device_id_type=MESH)
    pl.semaphore_wait(sem, len(peers))


def weight_round(p, cps, ws, d):
    got = []
    right = ((p.z + 9 - d) % 8) * 2 + p.c
    left = ((p.z + 7 + d) % 8) * 2 + p.c
    for w in ws:
        if d < 4:
            got.append((cps.go(w.at[:, right], w.at[:, right], p.zp()), w))
            got.append((cps.go(w.at[:, left], w.at[:, left], p.zm()), w))
        else:
            got.append((cps.go(w.at[0, right], w.at[0, right], p.zp()), w))
            got.append((cps.go(w.at[1, left], w.at[1, left], p.zm()), w))
    return got


def weight_finish(p, cps, ws, got, d):
    right = ((p.z + 8 - d) % 8) * 2 + p.c
    left = ((p.z + d) % 8) * 2 + p.c
    out = []
    for i, (cp, w) in enumerate(got):
        cp.wait_recv()
        if d < 4:
            slot = right if i % 2 == 0 else left
            out.append(cps.go(w.at[:, slot], w.at[:, slot], p.sib()))
        elif i % 2 == 1:
            out.append(cps.go(w.at[:, right], w.at[:, right], p.sib()))
    return out


def gather_hidden(ht, gate, up, down, xt, wg, wu, wd, send, recv, loc):
    p = Place()
    peers = [p.tens(o)[1] for o in range(1, 8)] + [p.xpart(), p.zp(), p.zm(), p.sib()]
    barrier(peers)
    cps = Copies(send, recv)
    ws = (wg, wu, wd)
    slot = p.z * 2 + p.c
    mine = pl.ds(pl.multiple_of(p.x * FFO, 128), FFP)
    other = pl.ds(pl.multiple_of((1 - p.x) * FFO, 128), FFP)
    swaps = [cps.go(a.at[:, other], w.at[p.x, slot], p.xpart()) for a, w in zip((gate, up, down), ws)]
    locs = [pltpu.make_async_copy(a.at[:, mine], w.at[p.x, slot], loc.at[i])
            for i, (a, w) in enumerate(zip((gate, up, down), ws))]
    rows = pl.ds(pl.multiple_of(p.t * 288, 32), 288)
    locs.append(pltpu.make_async_copy(ht, xt.at[rows], loc.at[3]))
    for cp in locs:
        cp.start()
    hid = [cps.go(ht, xt.at[rows], p.tens(o)[1]) for o in range(1, 8)]
    for cp in locs:
        cp.wait()
    for cp in swaps:
        cp.wait_recv()
    got = weight_round(p, cps, ws, 1)
    sib = [cps.go(w.at[:, slot], w.at[:, slot], p.sib()) for w in ws]
    sib += weight_finish(p, cps, ws, got, 1)
    for cp in hid + sib:
        cp.wait_recv()
    cps.drain_sends()


def exchange_kv(stay, go, q, kv, qa, send, recv, loc):
    p = Place()
    quads = [p.quad(o) for o in range(1, 4)]
    barrier([d for _, _, d in quads] + [p.zp(), p.zm(), p.sib()])
    cps = Copies(send, recv)
    slot = p.z * 2 + p.c
    locs = [pltpu.make_async_copy(stay, kv.at[p.yb, slot], loc.at[0]),
            pltpu.make_async_copy(q, qa.at[p.x * 2 + p.yb], loc.at[1])]
    for cp in locs:
        cp.start()
    pair = cps.go(go, kv.at[p.yb, slot], quads[0][2])
    qs = [cps.go(q, qa.at[p.x * 2 + p.yb], d) for _, _, d in quads]
    for cp in locs:
        cp.wait()
    pair.wait_recv()
    got = weight_round(p, cps, (kv,), 1)
    sib = [cps.go(kv.at[:, slot], kv.at[:, slot], p.sib())]
    for d in range(1, 5):
        for cp, _ in got:
            cp.wait_recv()
        nxt = weight_round(p, cps, (kv,), d + 1) if d < 4 else []
        right = ((p.z + 8 - d) % 8) * 2 + p.c
        left = ((p.z + d) % 8) * 2 + p.c
        sib.append(cps.go(kv.at[:, right], kv.at[:, right], p.sib()))
        if d < 4:
            sib.append(cps.go(kv.at[:, left], kv.at[:, left], p.sib()))
        got = nxt
    for cp in qs + sib:
        cp.wait_recv()
    cps.drain_sends()


def weight_tail(p, cps, ws, d):
    got = weight_round(p, cps, ws, d)
    return weight_finish(p, cps, ws, got, d)


def exchange_partials(part, wg0, wu0, wd0, rx, wg, wu, wd, send, recv):
    p = Place()
    quads = [p.quad(o) for o in range(1, 4)]
    barrier([d for _, _, d in quads] + [p.zp(), p.zm(), p.sib()])
    cps = Copies(send, recv)
    ex = [cps.go(part.at[x * 2 + yb], rx.at[o], d) for o, (x, yb, d) in enumerate(quads)]
    sib = weight_tail(p, cps, (wg, wu, wd), 2)
    for cp in ex + sib:
        cp.wait_recv()
    cps.drain_sends()


def scatter_tensor(o_ref, wg0, wu0, wd0, rx, wg, wu, wd, send, recv):
    p = Place()
    tens = [p.tens(o) for o in range(1, 8)]
    barrier([d for _, d in tens] + [p.zp(), p.zm(), p.sib()])
    cps = Copies(send, recv)
    ex = [cps.go(o_ref.at[t], rx.at[i], d) for i, (t, d) in enumerate(tens)]
    sib = weight_tail(p, cps, (wg, wu, wd), 3)
    for cp in ex + sib:
        cp.wait_recv()
    cps.drain_sends()


def gather_plane(f_ref, wg0, wu0, wd0, xa, wg, wu, wd, send, recv, loc):
    p = Place()
    plane = [p.plane(o) for o in range(1, 16)]
    barrier([d for _, d in plane] + [p.zp(), p.zm(), p.sib()])
    cps = Copies(send, recv)
    own = p.x * 8 + p.t
    lc = pltpu.make_async_copy(f_ref, xa.at[own], loc.at[0])
    lc.start()
    ex = [cps.go(f_ref, xa.at[own], d) for _, d in plane]
    sib = weight_tail(p, cps, (wg, wu, wd), 4)
    for cp in ex + sib:
        cp.wait_recv()
    lc.wait()
    cps.drain_sends()


def scatter_plane(y_ref, rx, send, recv):
    p = Place()
    plane = [p.plane(o) for o in range(1, 16)]
    barrier([d for _, d in plane])
    cps = Copies(send, recv)
    ex = [cps.go(y_ref.at[j], rx.at[i], d) for i, (j, d) in enumerate(plane)]
    for cp in ex:
        cp.wait_recv()
    cps.drain_sends()


def gather_rows(f_ref, xa, send, recv, loc):
    p = Place()
    tens = [p.tens(o) for o in range(1, 8)]
    barrier([d for _, d in tens])
    cps = Copies(send, recv)
    lc = pltpu.make_async_copy(f_ref, xa.at[p.t], loc.at[0])
    lc.start()
    ex = [cps.go(f_ref, xa.at[p.t], d) for _, d in tens]
    for cp in ex:
        cp.wait_recv()
    lc.wait()
    cps.drain_sends()


def call(body, cid, ins, in_specs, outs, out_specs, n, n_loc=0, aliases=None):
    scratch = [pltpu.SemaphoreType.DMA((n,)), pltpu.SemaphoreType.DMA((n,))]
    if n_loc:
        scratch.append(pltpu.SemaphoreType.DMA((n_loc,)))
    return pl.pallas_call(
        body,
        out_shape=[jax.ShapeDtypeStruct(s, bf16) for s in outs],
        in_specs=in_specs,
        out_specs=out_specs,
        scratch_shapes=scratch,
        input_output_aliases=aliases or {},
        compiler_params=pltpu.CompilerParams(collective_id=cid, has_side_effects=True),
        name=body.__name__,
    )(*ins)


def attend(flags, sel, qa, kv, qinfo, ktag, out, acc, den):
    for qb in range(4):
        x, blk = qb // 2, qb % 2
        rows = pl.ds(blk * 128, 128)
        acc[...] = jnp.zeros_like(acc)
        den[...] = jnp.zeros_like(den)

        def step(k, carry):
            @pl.when(flags[qb * 16 + k] != 0)
            def _():
                qt = jnp.concatenate([qa[2 * x, rows, :], qa[2 * x + 1, rows, :]], axis=0)
                score = lax.dot_general(qt, kv[0, k], (((1,), (1,)), ((), ())), preferred_element_type=f32)
                capped = SOFT_CAP * jnp.tanh(score * (0.0625 / SOFT_CAP))
                tag = qinfo[0, pl.ds(x * 256 + blk * 128, 128), :]
                start = qinfo[1, pl.ds(x * 256 + blk * 128, 128), :]
                kt = ktag[k]
                ok = (kt <= tag) & (kt >= start)
                weight = jnp.exp(capped)
                weight = jnp.concatenate(
                    [jnp.where(ok, weight[:128], 0.0), jnp.where(ok, weight[128:], 0.0)], axis=0
                ).astype(bf16)
                den[...] += weight.astype(f32)
                acc[...] += jnp.dot(weight, kv[1, k], preferred_element_type=f32)
            return carry

        lax.fori_loop(0, 16, step, 0)
        total = jnp.sum(den[...], axis=1, keepdims=True)
        high = total.astype(bf16).astype(f32)
        lane = lax.broadcasted_iota(jnp.int32, (256, 128), 1)
        both = jnp.where(lane < 64, high, total - high).astype(bf16)
        num = acc[...].astype(bf16)
        for h in range(2):
            out[2 * x + h, rows, 0:256] = num[h * 128:(h + 1) * 128]
            out[2 * x + h, rows, 256:384] = both[h * 128:(h + 1) * 128]
    for x in range(2):
        for j in range(2):
            k = sel[x * 2 + j]
            keep = jnp.where(k >= 0, 1.0, 0.0)
            at = jnp.maximum(k, 0)
            for part in range(2):
                picked = jnp.where(keep > 0, kv[part, at].astype(f32), 0.0)
                out[2 * x + part, pl.ds(j * 128, 128), 384:640] = picked.astype(bf16)


def row_norm(values, gain_vec):
    values = values.astype(f32)
    scale_vec = lax.rsqrt(jnp.mean(values * values, axis=-1, keepdims=True) + EPS)
    return values * scale_vec * gain_vec


def starts_of(tags, lengths):
    e0 = lengths[0]
    e1 = e0 + lengths[1]
    e2 = e1 + lengths[2]
    return jnp.where(tags >= e2, e2, jnp.where(tags >= e1, e1, jnp.where(tags >= e0, e0, 0)))


def spin(values, cosine, sine):
    half_dim = values.shape[-1] // 2
    a = values[:, :half_dim]
    b = values[:, half_dim:]
    return jnp.concatenate([a * cosine - b * sine, b * cosine + a * sine], axis=1)


def body(
    hidden, attn_gain, query_weight, kv_weight, out_weight, post_gain, ff_gain, ff_post_gain,
    gate_weight, up_weight, down_weight_t, next_gain, next_query_weight, next_kv_weight,
    lengths, pair_owner, page_table,
):
    p = Place()
    is_key = p.yb == 0
    local = jnp.arange(128, dtype=jnp.int32)
    ids = jnp.arange(32, dtype=jnp.int32)

    def pairs(idx):
        return jnp.sum(jnp.where(ids[None, :] == idx[:, None], pair_owner[None, :], 0), axis=1)

    qs = jnp.stack([p.z * 2 + p.c, 16 + p.z * 2 + p.c])
    qpair = pairs(qs)
    qblock = jnp.stack([qpair, 63 - qpair], axis=1).reshape(4)
    qtags = (qblock[:, None] * 128 + local[None, :]).reshape(512)
    qstart = starts_of(qtags, lengths)
    qinfo = jnp.stack([qtags, qstart])[:, :, None]
    kpair = pairs(p.x * 16 + jnp.arange(16, dtype=jnp.int32))
    kblock = jnp.where(is_key, kpair, 63 - kpair)
    ktag = (kblock[:, None] * 128 + local[None, :])[:, None, :]
    qfirst = starts_of(qblock * 128, lengths)
    flags = ((kblock[None, :] <= qblock[:, None]) & (kblock[None, :] * 128 + 127 >= qfirst[:, None])).astype(jnp.int32).reshape(64)
    pages = (2 * qs[:, None] + jnp.arange(2, dtype=jnp.int32)[None, :]).reshape(4)
    wanted = jnp.sum(jnp.where(page_table[None, :] == pages[:, None], jnp.arange(64, dtype=jnp.int32)[None, :], 0), axis=1)
    sel = jnp.sum(jnp.where(kblock[None, :] == wanted[:, None], jnp.arange(1, 17, dtype=jnp.int32)[None, :], 0), axis=1) - 1

    tags = lax.dynamic_slice_in_dim(qtags, p.x * 256, 256, 0)
    position = tags - lax.dynamic_slice_in_dim(qstart, p.x * 256, 256, 0)
    freq_vec = 10000.0 ** (-jnp.arange(128, dtype=f32) / 128)
    angles = position.astype(f32)[:, None] * freq_vec[None, :]
    cosine, sine = jnp.cos(angles), jnp.sin(angles)

    wshape = (2, 16, 72, FFP)
    xt, wg, wu, wd = call(
        gather_hidden, 1, (hidden.T, gate_weight, up_weight, down_weight_t), [VM] * 4,
        [(2304, 256), wshape, wshape, wshape], [VM, AN, AN, AN], 32, 4,
    )
    full_hidden = xt.T
    attn_input = row_norm(full_hidden, attn_gain).astype(bf16)
    queries = spin(jnp.dot(attn_input, query_weight, preferred_element_type=f32), cosine, sine).astype(bf16)
    own_proj = jnp.dot(attn_input, kv_weight, preferred_element_type=f32)
    own_part = jnp.where(is_key, spin(own_proj, cosine, sine), own_proj).astype(bf16)
    stay = jnp.where(is_key, own_part[:128], own_part[128:])
    go = jnp.where(is_key, own_part[128:], own_part[:128])
    kv, qa = call(
        exchange_kv, 2, (stay, go, queries), [VM] * 3, [(2, 16, 128, 256), (4, 256, 256)], [VM, VM], 24, 2,
    )
    part = pl.pallas_call(
        attend,
        out_shape=jax.ShapeDtypeStruct((4, 256, 640), bf16),
        in_specs=[pl.BlockSpec(memory_space=pltpu.SMEM)] * 2 + [VM] * 4,
        out_specs=VM,
        scratch_shapes=[pltpu.VMEM((256, 256), f32), pltpu.VMEM((256, 128), f32)],
        name="attend",
    )(flags, sel, qa, kv, qinfo, ktag)
    rx, wg, wu, wd = call(
        exchange_partials, 3, (part, wg, wu, wd), [VM, AN, AN, AN],
        [(3, 256, 640), wshape, wshape, wshape], [VM, AN, AN, AN], 16, 0, {1: 1, 2: 2, 3: 3},
    )
    mine = lax.dynamic_index_in_dim(part, p.x * 2 + p.yb, 0, keepdims=False).astype(f32)
    whole = mine + rx[0].astype(f32) + rx[1].astype(f32) + rx[2].astype(f32)
    kv_pages = whole[:, 384:640].astype(bf16).reshape(2, 128, 256)
    denominator = jnp.sum(whole[:, 256:384], axis=1, keepdims=True) * (1.0 / 64)
    attended = (whole[:, :256] / denominator).astype(bf16)
    partial = jnp.dot(attended, out_weight, preferred_element_type=f32).astype(bf16).reshape(8, 32, 2304)
    rx, wg, wu, wd = call(
        scatter_tensor, 4, (partial, wg, wu, wd), [VM, AN, AN, AN],
        [(7, 32, 2304), wshape, wshape, wshape], [VM, AN, AN, AN], 20, 0, {1: 1, 2: 2, 3: 3},
    )
    mine = lax.dynamic_index_in_dim(partial, p.t, 0, keepdims=False).astype(f32)
    attn_sum = mine + jnp.sum(rx.astype(f32), axis=0)
    own_hidden = lax.dynamic_slice_in_dim(full_hidden, p.t * 32, 32, 0).astype(f32)
    middle = (own_hidden + row_norm(attn_sum, post_gain)).astype(bf16)
    ff_input = row_norm(middle, ff_gain).astype(bf16)
    xa, wg, wu, wd = call(
        gather_plane, 5, (ff_input, wg, wu, wd), [VM, AN, AN, AN],
        [(16, 32, 2304), wshape, wshape, wshape], [VM, AN, AN, AN], 26, 1, {1: 1, 2: 2, 3: 3},
    )
    rows = xa.reshape(512, 2304)
    gate_val = jnp.dot(rows, wg.reshape(2304, FFP), preferred_element_type=f32)
    up_val = jnp.dot(rows, wu.reshape(2304, FFP), preferred_element_type=f32)
    column = jnp.arange(FFP, dtype=jnp.int32)
    keep = (p.x == 0) | (column >= FFP - FFO)
    inner = jnp.where(keep[None, :], jax.nn.gelu(gate_val, approximate=True) * up_val, 0.0).astype(bf16)
    ff_partial = lax.dot_general(
        inner, wd.reshape(2304, FFP), (((1,), (1,)), ((), ())), preferred_element_type=f32
    ).astype(bf16).reshape(16, 32, 2304)
    (rx,) = call(scatter_plane, 6, (ff_partial,), [VM], [(15, 32, 2304)], [VM], 15)
    mine = lax.dynamic_index_in_dim(ff_partial, p.x * 8 + p.t, 0, keepdims=False).astype(f32)
    ff_sum = mine + jnp.sum(rx.astype(f32), axis=0)
    own_final = (middle.astype(f32) + row_norm(ff_sum, ff_post_gain)).astype(bf16)
    (fr,) = call(gather_rows, 7, (own_final,), [VM], [(8, 32, 2304)], [VM], 7, 1)
    final_rows = fr.reshape(256, 2304)
    next_input = row_norm(final_rows, next_gain).astype(bf16)
    hidden_out = lax.dynamic_slice_in_dim(final_rows, p.t * 288, 288, 1)
    next_query = spin(jnp.dot(next_input, next_query_weight, preferred_element_type=f32), cosine, sine).astype(bf16)
    next_proj = jnp.dot(next_input, next_kv_weight, preferred_element_type=f32)
    next_kv = jnp.where(is_key, spin(next_proj, cosine, sine), next_proj).astype(bf16)
    return (hidden_out, next_query, next_kv, kv_pages)


def solution(mesh):
    wide = P("seq", "tensor")
    cols = P(None, "tensor")
    in_specs = (wide, P(), cols, cols, P("tensor", None), P(), P(), P(), wide, wide, wide, P(), cols, cols, P(), P(), P())
    out_specs = (wide, wide, wide, P("seq", None, "tensor"))
    return jax.shard_map(body, mesh=mesh, in_specs=in_specs, out_specs=out_specs, check_vma=False)
```

time: 711 us -> 296 us (0.42)
  waiting for transfers between devices: 595 us -> 0 us
  Pallas kernels: 0 us -> 234 us
  blocking collectives: 40 us -> 0 us
  matrix products: 40.1 us -> 21.9 us
  between operations: 17 us -> 2.97 us
  other arithmetic: 13.6 us -> 25.4 us
    all_gather x6 -> x0, waiting for transfers between devices: 425 us -> none  [the longest x1 90.3 us: body(): lax.all_gather(down_weight_t, 'seq', axis=0, tiled=True)]
    pallas_call x0 -> x8, Pallas kernels: none -> 234 us  [the longest x7 227 us: call(): pl.pallas_call(body, out_shape=[jax.ShapeDtypeStruct(s, bf16) for s in ou...]
    psum x2 -> x0, waiting for transfers between devices: 162 us -> none  [the longest x1 86.2 us: body(): attn_sum = lax.psum(attn_partial, 'tensor')]
    all_gather x1 -> x0, blocking collectives: 40 us -> none  [body(): key_tags = lax.all_gather(tags, 'seq', axis=0, tiled=True)]
    dot_general x9 -> x7, matrix products: 40.1 us -> 21.9 us  [the longest x1 9.67 us: body(): lax.dot_general(inner, wd.reshape(2304, FFP), (((1,), (1,)), ((), ())), p...]
  transfers between devices with their start and end apart: 9 -> 0, of which waited for: 9 -> 0; matrix products, arithmetic and copies ran while one was open for 4% -> 0% of each run, Pallas kernels for 0% -> 0%
where the time goes in v1:
time: 296 us; the launch traced here: 290 us
  Pallas kernels  234 us (79%)
  other arithmetic  25.4 us (9%)
  matrix products  21.9 us (7%)
  local copies, waits for them, and re-layouts  5.71 us (2%)
  between operations  2.97 us (1%)
    pallas_call x7, Pallas kernels, call(): pl.pallas_call(body, out_shape=[jax.ShapeDtypeStruct(s, bf16) for s in ou...  227 us
    dot_general x1, matrix products, body(): lax.dot_general(inner, wd.reshape(2304, FFP), (((1,), (1,)), ((), ())), p...  9.67 us
    pallas_call x1, Pallas kernels, body(): pl.pallas_call(attend, out_shape=jax.ShapeDtypeStruct((4, 256, 640), bf16...  7.72 us
    reduce_sum x5, other arithmetic, row_norm(): jnp.mean(values * values, axis=-1, keepdims=True) + EPS  6.57 us

profile of v1, /device:TPU:4, one launch (start us, length us, event | category | flops | bytes accessed | tf_op | source)
XLA Modules:
  0.0 290.4 jit_solution(4611033247075387628)
XLA Ops:
  4.5 1.4 fusion.65
  11.4 1.0 copy.64.qinfo
  12.4 33.4 %gather_hidden.1 = (bf16[2304,256]{1,0:T(8,128)(2,1)}, bf16[2,16,72,640]{3,2,1,0:T(8,128)(2,1)}, bf16[2,16,72,640]{3,2,1,0:T(8,128)(2,1)}, bf16[2,16,72,640]{3,2,1,0:T(8,128)(2,1)}) custom-call(bf16[288,256]{1,0:T(8,128)(2,1)} %bitcast.61, bf16[72,1152]{1,0:T(8,128)(2,1)} %gate.1, bf16[72,1152]{1,0:T(8,128)(2,1)} %up.1, bf16[72,1152]{1,0:T(8,128)(2,1)} %down.1), custom_call_target="tpu_custom_call" | custom-call | tf_op jit(solution)/shard_map/gather_hidden/pallas_call | solution.py:257
  45.9 1.6 fusion
  47.5 2.7 fusion.16
  54.4 30.0 %exchange_kv.1 = (bf16[2,16,128,256]{3,2,1,0:T(8,128)(2,1)}, bf16[4,256,256]{2,1,0:T(8,128)(2,1)}) custom-call(bf16[128,256]{1,0:T(8,128)(2,1)} %get-tuple-element.55.stay, bf16[128,256]{1,0:T(8,128)(2,1)} %get-tuple-element.54.go, bf16[256,256]{1,0:T(8,128)(2,1)} %pad_maximum_fusion.q), custom_call_target="tpu_custom_call" | custom-call | tf_op jit(solution)/shard_map/exchange_kv/pallas_call | solution.py:257
  84.4 7.7 %attend.1.part = bf16[4,256,640]{2,1,0:T(8,128)(2,1)} custom-call(s32[64]{0:T(128)} %reshape.295.flags, s32[4]{0:T(128)} %broadcast_add_fusion.sel, bf16[4,256,256]{2,1,0:T(8,128)(2,1)} %get-tuple-element.23.qa, bf16[2,16,128,256]{3,2,1,0:T(8,128)(2,1)} %get-tuple-element.24.kv, s32[2,512,1]{2,1,0:T(8,128)} %copy.64.qinfo, s32[16,1,128]{2,1,0:T(1,128)} %iota_add_fusion.ktag), custom_call_target="tpu_custom_call" | custom-call | tf_op jit(solution)/shard_map/attend/pallas_call | solution.py:382
  92.1 23.1 %exchange_partials.1 = (bf16[3,256,640]{2,1,0:T(8,128)(2,1)}, bf16[2,16,72,640]{3,2,1,0:T(8,128)(2,1)}, bf16[2,16,72,640]{3,2,1,0:T(8,128)(2,1)}, bf16[2,16,72,640]{3,2,1,0:T(8,128)(2,1)}) custom-call(bf16[4,256,640]{2,1,0:T(8,128)(2,1)} %attend.1.part, ...), custom_call_target="tpu_custom_call", output_to_operand_aliasing={{1}: (1, {}), {2}: (2, {}), {3}: (3, {})} | custom-call | tf_op jit(solution)/shard_map/exchange_partials/pallas_call | solution.py:257
  115.2 1.4 add_bitcast_fusion
  117.4 1.6 convolution_convert_fusion.1
  119.1 22.8 %scatter_tensor.1 = (bf16[7,32,2304]{2,1,0:T(8,128)(2,1)}, bf16[2,16,72,640]{3,2,1,0:T(8,128)(2,1)}, bf16[2,16,72,640]{3,2,1,0:T(8,128)(2,1)}, bf16[2,16,72,640]{3,2,1,0:T(8,128)(2,1)}) custom-call(bf16[8,32,2304]{2,1,0:T(8,128)(2,1)} %bitcast.52, ...), custom_call_target="tpu_custom_call", output_to_operand_aliasing={{1}: (1, {}), {2}: (2, {}), {3}: (3, {})} | custom-call | tf_op jit(solution)/shard_map/scatter_tensor/pallas_call | solution.py:257
  141.9 1.4 convert_reduce_fusion.1
  143.3 1.1 multiply_reduce_fusion.2
  144.4 1.2 fusion.18
  146.3 45.4 %gather_plane.1 = (bf16[16,32,2304]{2,1,0:T(8,128)(2,1)}, bf16[2,16,72,640]{3,2,1,0:T(8,128)(2,1)}, bf16[2,16,72,640]{3,2,1,0:T(8,128)(2,1)}, bf16[2,16,72,640]{3,2,1,0:T(8,128)(2,1)}) custom-call(bf16[32,2304]{1,0:T(8,128)(2,1)} %fusion.20.f_ref, ...), custom_call_target="tpu_custom_call", output_to_operand_aliasing={{1}: (1, {}), {2}: (2, {}), {3}: (3, {})} | custom-call | tf_op jit(solution)/shard_map/gather_plane/pallas_call | solution.py:257
  191.7 4.5 %fusion.66 = f32[512,640]{1,0:T(8,128)S(1)} fusion(bf16[512,2304]{1,0:T(8,128)(2,1)} %bitcast.66, bf16[2304,640]{1,0:T(8,128)(2,1)} %bitcast.49), kind=kOutput, calls=%fused_computation.130 | convolution fusion | flops 1509949440 | bytes 6619136 | tf_op jit(solution)/shard_map/dot_general | solution.py:414
  196.3 9.7 %convolution_convert_fusion = bf16[512,2304]{1,0:T(8,128)(2,1)} fusion(bf16[2304,640]{1,0:T(8,128)(2,1)} %bitcast.51, bf16[512,2304]{1,0:T(8,128)(2,1)} %bitcast.67, bf16[2304,640]{1,0:T(8,128)(2,1)} %bitcast.50, f32[512,640]{1,0:T(8,128)S(1)} %fusion.66, pred[640]{0:T(1024)(128)(4,1)S(1)} %fusion.56), kind=kOutput, calls=%fused_computation | convolution fusion | flops 3024683008 | bytes 11928192 | tf_op jit(solution)/shard_map/dot_general | solution.py:419
  206.0 47.7 %scatter_plane.1 = bf16[15,32,2304]{2,1,0:T(8,128)(2,1)} custom-call(bf16[16,32,2304]{2,1,0:T(8,128)(2,1)} %bitcast.58), custom_call_target="tpu_custom_call" | custom-call | tf_op jit(solution)/shard_map/scatter_plane/pallas_call | solution.py:257
  253.7 2.0 convert_reduce_fusion
  255.7 1.1 multiply_reduce_fusion.1
  256.8 1.7 fusion.21.f_ref
  258.4 24.3 %gather_rows.1 = bf16[8,32,2304]{2,1,0:T(8,128)(2,1)} custom-call(bf16[32,2304]{1,0:T(8,128)(2,1)} %fusion.21.f_ref), custom_call_target="tpu_custom_call" | custom-call | tf_op jit(solution)/shard_map/gather_rows/pallas_call | solution.py:257
  282.8 1.7 multiply_reduce_fusion
  285.5 1.9 fusion.12
  (70 shorter events, 17.1 us)
Async XLA Ops:
  0.6 116.8 %copy-start = (bf16[256,2304]{1,0:T(8,128)(2,1)S(1)}, bf16[256,2304]{1,0:T(8,128)(2,1)}, u32[]{:S(2)}) copy-start(bf16[256,2304]{1,0:T(8,128)(2,1)} %param.21) | copy-start | bytes 3538948
  0.7 46.8 %copy-start.8 = (f32[2304]{0:T(1024)S(1)}, f32[2304]{0:T(1024)}, u32[]{:S(2)}) copy-start(f32[2304]{0:T(1024)} %param.18) | copy-start | bytes 27652
  47.5 4.0 %copy-start.2 = (bf16[2304,256]{1,0:T(8,128)(2,1)S(1)}, bf16[2304,256]{1,0:T(8,128)(2,1)}, u32[]{:S(2)}) copy-start(bf16[2304,256]{1,0:T(8,128)(2,1)} %get-tuple-element.22) | copy-start | bytes 3538948
  47.5 4.0 %copy-start.6 = (bf16[2304,256]{1,0:T(8,128)(2,1)S(1)}, bf16[2304,256]{1,0:T(8,128)(2,1)}, u32[]{:S(2)}) copy-start(bf16[2304,256]{1,0:T(8,128)(2,1)} %param.19) | copy-start | bytes 3538948
  141.9 2.5 copy-start.4
  141.9 3.6 %copy-start.3 = (f32[2304]{0:T(1024)S(1)}, f32[2304]{0:T(1024)}, u32[]{:S(2)}) copy-start(f32[2304]{0:T(1024)} %param.23) | copy-start | bytes 27652
  253.7 3.1 %copy-start.5 = (f32[2304]{0:T(1024)S(1)}, f32[2304]{0:T(1024)}, u32[]{:S(2)}) copy-start(f32[2304]{0:T(1024)} %param.24) | copy-start | bytes 27652
  258.4 27.0 %copy-start.9 = (f32[2304]{0:T(1024)S(1)}, f32[2304]{0:T(1024)}, u32[]{:S(2)}) copy-start(f32[2304]{0:T(1024)} %param.28) | copy-start | bytes 27652
  282.8 1.8 copy-start.1
  285.5 1.9 copy-start.7

commit v2 on v1

v2 whole, which is shorter than its diff:
```python
import functools

import jax
import jax.numpy as jnp
from jax import lax
from jax.experimental import pallas as pl
from jax.experimental.pallas import tpu as pltpu
from jax.sharding import PartitionSpec as P

EPS = 1e-06
SOFT_CAP = 50.0
MESH = pl.DeviceIdType.MESH
VM = pl.BlockSpec(memory_space=pltpu.VMEM)
AN = pl.BlockSpec(memory_space=pl.ANY)
FFP = 640
FFO = 512
bf16 = jnp.bfloat16
f32 = jnp.float32


class Place:
    def __init__(self):
        self.s = lax.axis_index("seq")
        self.t = lax.axis_index("tensor")
        self.x = self.s // 16
        self.z = (self.s // 2) % 8
        self.c = self.s % 2
        self.yb = self.t % 2
        self.X = self.x * 2 + self.t // 4
        self.Y = self.t % 4

    def grid(self, X, Y):
        return self.dev(self.seq(X // 2, self.z, self.c), (X % 2) * 4 + Y)

    def near(self, dim, sign, nx):
        if dim == 1:
            return self.grid(self.X, (self.Y + 4 + sign) % 4)
        if nx == 2:
            return self.dev(self.s, (self.t + 4) % 8)
        return self.grid((self.X + 4 + sign) % 4, self.Y)

    def around(self, nx):
        out = [self.near(1, 1, nx), self.near(1, -1, nx), self.near(0, 1, nx)]
        return out + ([self.near(0, -1, nx)] if nx == 4 else [])

    def seq(self, x, z, c):
        return x * 16 + z * 2 + c

    def dev(self, s, t):
        return {"seq": s, "tensor": t}

    def zp(self):
        return self.dev(self.seq(self.x, (self.z + 1) % 8, self.c), self.t)

    def zm(self):
        return self.dev(self.seq(self.x, (self.z + 7) % 8, self.c), self.t)

    def sib(self):
        return self.dev(self.seq(self.x, self.z, 1 - self.c), self.t)

    def xpart(self):
        return self.dev(self.seq(1 - self.x, self.z, self.c), self.t)

    def quad(self, o):
        dx, dy = o // 2, o % 2
        x = (self.x + dx) % 2
        yb = (self.yb + dy) % 2
        return x, yb, self.dev(self.seq(x, self.z, self.c), self.t - self.yb + yb)

    def tens(self, o):
        t = (self.t + o) % 8
        return t, self.dev(self.s, t)

    def plane(self, o):
        j = (self.x * 8 + self.t + o) % 16
        x, t = j // 8, j % 8
        return j, self.dev(self.seq(x, self.z, self.c), t)


class Copies:
    def __init__(self, send, recv):
        self.send, self.recv, self.n, self.live = send, recv, 0, []

    def make(self, src, dst, dev):
        i = self.n
        self.n += 1
        return pltpu.make_async_remote_copy(
            src_ref=src, dst_ref=dst, send_sem=self.send.at[i], recv_sem=self.recv.at[i],
            device_id=dev, device_id_type=MESH,
        )

    def go(self, src, dst, dev):
        cp = self.make(src, dst, dev)
        cp.start()
        self.live.append(cp)
        return cp

    def drain_sends(self):
        for cp in self.live:
            cp.wait_send()


def barrier(peers):
    sem = pltpu.get_barrier_semaphore()
    for dev in peers:
        pl.semaphore_signal(sem, inc=1, device_id=dev, device_id_type=MESH)
    pl.semaphore_wait(sem, len(peers))


def gather_grid(p, cps, own, view, nx):
    size = (nx, 4)

    def send(h, a, b, sub, dim, sign):
        dx, dy = (a, b) if h == 0 else (b, a)
        dst = view(dx, dy, h, sub)
        return cps.go(own(h) if (a, b) == (0, 0) else dst, dst, p.near(dim, sign, nx))

    def spread(h, a, b, dim):
        return [send(h, a, b, None, dim, sign) for sign in ((1, -1) if size[dim] == 4 else (1,))]

    first = [spread(h, 0, 0, h) for h in range(2)]
    second = [{0: spread(h, 0, 0, 1 - h)} for h in range(2)]
    far = [[], []]
    last = []
    for i in range(2):
        for h in range(2):
            if i < len(first[h]):
                first[h][i].wait_recv()
                a = (-1, 1)[i]
                if size[h] == 4:
                    far[h].append(send(h, a, 0, i, h, -a))
                second[h][a] = spread(h, a, 0, 1 - h)

    def onward(h, a):
        for i, cp in enumerate(second[h][a]):
            cp.wait_recv()
            if size[1 - h] == 4:
                b = (-1, 1)[i]
                last.append(send(h, a, b, i, 1 - h, -b))

    for h in range(2):
        onward(h, 0)
    for h in range(2):
        if far[h]:
            for cp in far[h]:
                cp.wait_recv()
            second[h][2] = spread(h, 2, 0, 1 - h)
    for a in (-1, 1, 2):
        for h in range(2):
            if a in second[h]:
                onward(h, a)
    for cp in last:
        cp.wait_recv()


ROW = (slice(0, 16), slice(16, 32))
COL = (slice(0, 1152), slice(1152, 2304))


def reduce_line(p, cps, read, view, buf, dim, nx):
    size = (nx, 4)[dim]
    rp, rm, up, dn, bu, bd = buf
    plus, minus = p.near(dim, 1, nx), p.near(dim, -1, nx)
    if size == 2:
        cp = cps.go(view(1, None), rp, plus)

        def finish():
            cp.wait_recv()
            return read(0, None) + rp[...].astype(f32)

        return [finish]
    far0 = cps.go(view(2, 0), up, plus)
    far1 = cps.go(view(2, 1), dn, minus)
    near = [cps.go(view(1, 1), rp.at[:, ROW[1]], plus), cps.go(view(-1, 0), rm.at[:, ROW[0]], minus)]

    def relay():
        far0.wait_recv()
        bu[...] = (read(1, 0) + up[...].astype(f32)).astype(bf16)
        near.append(cps.go(bu, rp.at[:, ROW[0]], plus))
        far1.wait_recv()
        bd[...] = (read(-1, 1) + dn[...].astype(f32)).astype(bf16)
        near.append(cps.go(bd, rm.at[:, ROW[1]], minus))

    def finish():
        for cp in near:
            cp.wait_recv()
        return read(0, None) + rp[...].astype(f32) + rm[...].astype(f32)

    return [relay, finish]


def reduce_grid(p, cps, part, bufs, sums, nx):
    at = (p.X if nx == 4 else p.X % 2, p.Y)
    size = (nx, 4)

    def one(h):
        def view(d, sub):
            rows = slice(0, 32) if sub is None else ROW[sub]
            i = (at[1 - h] + size[1 - h] + d) % size[1 - h]
            return part.at[:, i, rows, COL[h]] if h == 0 else part.at[i, :, rows, COL[h]]

        def read(d, sub):
            return view(d, sub)[...].astype(f32)

        return reduce_line(p, cps, read, view, bufs[h][:6], 1 - h, nx)

    def two(h):
        def view(d, sub):
            rows = slice(0, 32) if sub is None else ROW[sub]
            i = (at[h] + size[h] + d) % size[h]
            return sums[h].at[pl.ds(i, 1), rows]

        def read(d, sub):
            return view(d, sub)[...].astype(f32)

        return reduce_line(p, cps, read, view, bufs[h][6:], h, nx)

    steps = [one(h) for h in range(2)]
    for h in range(2):
        if len(steps[h]) == 2:
            steps[h][0]()
    later = []
    for h in range(2):
        sums[h][...] = steps[h][-1]().astype(bf16)
        later.append(two(h))
    for h in range(2):
        if len(later[h]) == 2:
            later[h][0]()
    return [later[h][-1]()[0] for h in range(2)]


def reduce_scratch(nx):
    out = []
    for h in range(2):
        size = (nx, 4)
        for n, m in ((size[h], size[1 - h]), (1, size[h])):
            del m
            out += [pltpu.VMEM((n, 32, 1152), bf16)] * 2 + [pltpu.VMEM((n, 16, 1152), bf16)] * 4
        out.append(pltpu.VMEM((size[h], 32, 1152), bf16))
    return out


def reduce_bufs(refs):
    return [refs[0:12], refs[13:25]], [refs[12], refs[25]]


def normed(values, gain):
    return values * lax.rsqrt(jnp.mean(values * values, axis=1, keepdims=True) + EPS) * gain[...]


def weight_round(p, cps, ws, d):
    got = []
    right = ((p.z + 9 - d) % 8) * 2 + p.c
    left = ((p.z + 7 + d) % 8) * 2 + p.c
    for w in ws:
        if d < 4:
            got.append((cps.go(w.at[:, right], w.at[:, right], p.zp()), w))
            got.append((cps.go(w.at[:, left], w.at[:, left], p.zm()), w))
        else:
            got.append((cps.go(w.at[0, right], w.at[0, right], p.zp()), w))
            got.append((cps.go(w.at[1, left], w.at[1, left], p.zm()), w))
    return got


def weight_finish(p, cps, got, d):
    right = ((p.z + 8 - d) % 8) * 2 + p.c
    left = ((p.z + d) % 8) * 2 + p.c
    out = []
    for i, (cp, w) in enumerate(got):
        cp.wait_recv()
        if d < 4:
            slot = right if i % 2 == 0 else left
            out.append(cps.go(w.at[:, slot], w.at[:, slot], p.sib()))
        elif i % 2 == 1:
            out.append(cps.go(w.at[:, right], w.at[:, right], p.sib()))
    return out


def gather_hidden(ht, gate, up, down, xt, wg, wu, wd, send, recv, loc):
    p = Place()
    barrier(p.around(2) + [p.xpart(), p.zp(), p.zm(), p.sib()])
    cps = Copies(send, recv)
    ws = (wg, wu, wd)
    slot = p.z * 2 + p.c
    mine = pl.ds(pl.multiple_of(p.x * FFO, 128), FFP)
    other = pl.ds(pl.multiple_of((1 - p.x) * FFO, 128), FFP)
    swaps = [cps.go(a.at[:, other], w.at[p.x, slot], p.xpart()) for a, w in zip((gate, up, down), ws)]
    ring = [cps.go(a.at[:, mine], w.at[p.x, slot], dev) for a, w in zip((gate, up, down), ws)
            for dev in (p.zp(), p.zm())]
    locs = [pltpu.make_async_copy(a.at[:, mine], w.at[p.x, slot], loc.at[i])
            for i, (a, w) in enumerate(zip((gate, up, down), ws))]

    def view(dx, dy, h, sub):
        t = ((p.t // 4 + 2 + dx) % 2) * 4 + (p.Y + 4 + dy) % 4
        low, n = ((0, 144) if sub is None else ((0, 80), (80, 64))[sub])
        return xt.at[t, pl.ds(h * 144 + low, n)]

    locs.append(pltpu.make_async_copy(ht, xt.at[p.t], loc.at[3]))
    for cp in locs:
        cp.start()
    gather_grid(p, cps, lambda h: ht.at[pl.ds(h * 144, 144)], view, 2)
    for cp in swaps:
        cp.wait_recv()
    for w in ws:
        ring += [cps.go(w.at[1 - p.x, slot], w.at[1 - p.x, slot], dev) for dev in (p.zp(), p.zm())]
    for cp in locs:
        cp.wait()
    sib = [cps.go(w.at[:, slot], w.at[:, slot], p.sib()) for w in ws]
    right = ((p.z + 7) % 8) * 2 + p.c
    left = ((p.z + 1) % 8) * 2 + p.c
    for i in range(6):
        ring[i].wait_recv()
        ring[i + 6].wait_recv()
        w = ws[i // 2]
        at = right if i % 2 == 0 else left
        sib.append(cps.go(w.at[:, at], w.at[:, at], p.sib()))
    for cp in sib:
        cp.wait_recv()
    cps.drain_sends()


def exchange_kv(stay, go, q, kv, qa, send, recv, loc):
    p = Place()
    quads = [p.quad(o) for o in range(1, 4)]
    barrier([d for _, _, d in quads] + [p.zp(), p.zm(), p.sib()])
    cps = Copies(send, recv)
    slot = p.z * 2 + p.c
    parts = (p.yb, 1 - p.yb)
    pair = cps.go(go, kv.at[p.yb, slot], quads[0][2])
    got = [[cps.go(stay, kv.at[p.yb, slot], p.zp()), cps.go(stay, kv.at[p.yb, slot], p.zm())]]
    locs = [pltpu.make_async_copy(stay, kv.at[p.yb, slot], loc.at[0]),
            pltpu.make_async_copy(q, qa.at[p.x * 2 + p.yb], loc.at[1])]
    for cp in locs:
        cp.start()
    sib = [cps.go(stay, kv.at[p.yb, slot], p.sib())]
    qs = [cps.go(q, qa.at[p.x * 2 + p.yb], d) for _, _, d in quads]
    pair.wait_recv()
    own = kv.at[1 - p.yb, slot]
    got.append([cps.go(own, own, p.zp()), cps.go(own, own, p.zm())])
    sib.append(cps.go(own, own, p.sib()))
    for d in range(1, 5):
        right = ((p.z + 8 - d) % 8) * 2 + p.c
        left = ((p.z + d) % 8) * 2 + p.c
        nxt = [[], []]
        for i, part in enumerate(parts):
            for side, cp in enumerate(got[i]):
                cp.wait_recv()
                if d < 4:
                    here = kv.at[part, (right, left)[side]]
                    if d < 3 or side == i:
                        nxt[i].append(cps.go(here, here, (p.zp(), p.zm())[side]))
                    sib.append(cps.go(here, here, p.sib()))
                else:
                    here = kv.at[part, right]
                    sib.append(cps.go(here, here, p.sib()))
        got = nxt
    for cp in locs:
        cp.wait()
    for cp in qs + sib:
        cp.wait_recv()
    cps.drain_sends()


def exchange_partials(num, den, wg0, wu0, wd0, rn, rd, wg, wu, wd, send, recv):
    p = Place()
    quads = [p.quad(o) for o in range(1, 4)]
    barrier([d for _, _, d in quads] + [p.zp(), p.zm(), p.sib()])
    cps = Copies(send, recv)
    ex = [cps.go(num.at[x * 2 + yb], rn.at[o], d) for o, (x, yb, d) in enumerate(quads)]
    ex += [cps.go(den.at[x * 2 + yb], rd.at[o], d) for o, (x, yb, d) in enumerate(quads)]
    got = weight_round(p, cps, (wg, wu, wd), 2)
    sib = weight_finish(p, cps, got, 2)
    for cp in ex + sib:
        cp.wait_recv()
    cps.drain_sends()


def mix_tensor(o_ref, hid, post_gain, ff_gain, wg0, wu0, wd0, mid, xa, wg, wu, wd, send, recv, loc, mine, *scratch):
    p = Place()
    barrier(p.around(4) + [p.zp(), p.zm(), p.sib()])
    cps = Copies(send, recv)
    ws = (wg, wu, wd)
    got = weight_round(p, cps, ws, 3)
    bufs, sums = reduce_bufs(scratch)
    total = jnp.concatenate(reduce_grid(p, cps, o_ref, bufs, sums, 2), axis=1)
    middle = (hid[...].astype(f32) + normed(total, post_gain)).astype(bf16)
    mid[...] = middle
    mine[...] = normed(middle.astype(f32), ff_gain).astype(bf16)
    lc = pltpu.make_async_copy(mine, xa.at[p.X, p.Y], loc.at[0])
    lc.start()
    sib = weight_finish(p, cps, got, 3)
    got = weight_round(p, cps, ws, 4)

    def view(dx, dy, h, sub):
        rows = slice(0, 32) if sub is None else ROW[sub]
        return xa.at[(p.X + 4 + dx) % 4, (p.Y + 4 + dy) % 4, rows, COL[h]]

    gather_grid(p, cps, lambda h: mine.at[:, COL[h]], view, 4)
    sib += weight_finish(p, cps, got, 4)
    for cp in sib:
        cp.wait_recv()
    lc.wait()
    cps.drain_sends()


def mix_plane(y_ref, mid, gain, xa, send, recv, loc, mine, *scratch):
    p = Place()
    barrier(p.around(4))
    cps = Copies(send, recv)
    bufs, sums = reduce_bufs(scratch)
    total = jnp.concatenate(reduce_grid(p, cps, y_ref, bufs, sums, 4), axis=1)
    mine[...] = (mid[...].astype(f32) + normed(total, gain)).astype(bf16)
    lc = pltpu.make_async_copy(mine, xa.at[p.t], loc.at[0])
    lc.start()

    def view(dx, dy, h, sub):
        rows = slice(0, 32) if sub is None else ROW[sub]
        return xa.at[((p.X + 2 + dx) % 2) * 4 + (p.Y + 4 + dy) % 4, rows, COL[h]]

    gather_grid(p, cps, lambda h: mine.at[:, COL[h]], view, 2)
    lc.wait()
    cps.drain_sends()


def call(body, cid, ins, in_specs, outs, out_specs, n, n_loc=0, aliases=None, extra=()):
    scratch = [pltpu.SemaphoreType.DMA((n,)), pltpu.SemaphoreType.DMA((n,))]
    if n_loc:
        scratch.append(pltpu.SemaphoreType.DMA((n_loc,)))
    return pl.pallas_call(
        body,
        out_shape=[s if isinstance(s, jax.ShapeDtypeStruct) else jax.ShapeDtypeStruct(s, bf16) for s in outs],
        in_specs=in_specs,
        out_specs=out_specs,
        scratch_shapes=scratch + list(extra),
        input_output_aliases=aliases or {},
        compiler_params=pltpu.CompilerParams(collective_id=cid, has_side_effects=True),
        name=body.__name__,
    )(*ins)


def attend(lengths, owner, table, qa, kv, out, out_den, out_page, acc, den):
    p = Place()
    e0 = lengths[0]
    e1 = e0 + lengths[1]
    e2 = e1 + lengths[2]

    def start_of(tag):
        return jnp.where(tag >= e2, e2, jnp.where(tag >= e1, e1, jnp.where(tag >= e0, e0, 0)))

    row = lax.broadcasted_iota(jnp.int32, (128, 128), 0)
    lane = lax.broadcasted_iota(jnp.int32, (128, 128), 1)

    def key_block(k):
        b = owner[p.x * 16 + k]
        return jnp.where(p.yb == 0, b, 63 - b)

    for qb in range(4):
        x, blk = qb // 2, qb % 2
        rows = pl.ds(blk * 128, 128)
        acc[...] = jnp.zeros_like(acc)
        den[...] = jnp.zeros_like(den)
        b = owner[x * 16 + p.z * 2 + p.c]
        q_block = b if blk == 0 else 63 - b
        first = start_of(q_block * 128)

        def step(k, carry):
            k_block = key_block(k)

            @pl.when((k_block <= q_block) & (k_block * 128 + 127 >= first))
            def _():
                qt = jnp.concatenate([qa[2 * x, rows, :], qa[2 * x + 1, rows, :]], axis=0)
                score = lax.dot_general(qt, kv[0, k], (((1,), (1,)), ((), ())), preferred_element_type=f32)
                capped = SOFT_CAP * jnp.tanh(score * (0.0625 / SOFT_CAP))
                tag = q_block * 128 + row
                kt = k_block * 128 + lane
                ok = (kt <= tag) & (kt >= start_of(tag))
                weight = jnp.exp(capped)
                weight = jnp.concatenate(
                    [jnp.where(ok, weight[:128], 0.0), jnp.where(ok, weight[128:], 0.0)], axis=0
                ).astype(bf16)
                den[...] += weight.astype(f32)
                acc[...] += jnp.dot(weight, kv[1, k], preferred_element_type=f32)
            return carry

        lax.fori_loop(0, 16, step, 0)
        total = lax.dot_general(
            jnp.ones((8, 128), f32), den[...], (((1,), (1,)), ((), ())),
            precision=lax.Precision.HIGHEST, preferred_element_type=f32,
        )
        num = acc[...].astype(bf16)
        for h in range(2):
            out[2 * x + h, rows, :] = num[h * 128:(h + 1) * 128]
            out_den[2 * x + h, :, blk * 128:(blk + 1) * 128] = total[:, h * 128:(h + 1) * 128]

    base = p.z * 4 + p.c * 2

    def look(i, found):
        page = table[i]
        return tuple(jnp.where(page == (n // 2) * 32 + base + n % 2, i, f) for n, f in enumerate(found))

    wanted = lax.fori_loop(0, 64, look, (jnp.int32(0),) * 4)

    def match(k, found):
        block = key_block(k)
        return tuple(jnp.where(block == w, k, f) for w, f in zip(wanted, found))

    chosen = lax.fori_loop(0, 16, match, (jnp.int32(-1),) * 4)
    for n in range(4):
        at = jnp.maximum(chosen[n], 0)
        for part in range(2):
            picked = jnp.where(chosen[n] >= 0, kv[part, at].astype(f32), 0.0)
            out_page[(n // 2) * 2 + part, pl.ds((n % 2) * 128, 128), :] = picked.astype(bf16)


def quad_route(dx, dy):
    route = []
    for s in range(32):
        for t in range(8):
            route.append((s * 8 + t, ((s + 16 * dx) % 32) * 8 + (t ^ dy)))
    return route


def row_norm(values, gain_vec):
    values = values.astype(f32)
    scale_vec = lax.rsqrt(jnp.mean(values * values, axis=-1, keepdims=True) + EPS)
    return values * scale_vec * gain_vec


def starts_of(tags, lengths):
    e0 = lengths[0]
    e1 = e0 + lengths[1]
    e2 = e1 + lengths[2]
    return jnp.where(tags >= e2, e2, jnp.where(tags >= e1, e1, jnp.where(tags >= e0, e0, 0)))


def spin(values, cosine, sine):
    half_dim = values.shape[-1] // 2
    a = values[:, :half_dim]
    b = values[:, half_dim:]
    return jnp.concatenate([a * cosine - b * sine, b * cosine + a * sine], axis=1)


def body(
    hidden, attn_gain, query_weight, kv_weight, out_weight, post_gain, ff_gain, ff_post_gain,
    gate_weight, up_weight, down_weight_t, next_gain, next_query_weight, next_kv_weight,
    lengths, pair_owner, page_table,
):
    p = Place()
    is_key = p.yb == 0
    owned = jnp.sum(jnp.where(jnp.arange(32, dtype=jnp.int32) == p.s, pair_owner, 0))
    local = jnp.arange(256, dtype=jnp.int32)
    tags = jnp.where(local < 128, owned * 128 + local, (63 - owned) * 128 + local - 128)
    position = tags - starts_of(tags, lengths)
    freq_vec = 10000.0 ** (-jnp.arange(128, dtype=f32) / 128)
    angles = position.astype(f32)[:, None] * freq_vec[None, :]
    cosine, sine = jnp.cos(angles), jnp.sin(angles)

    wshape = (2, 16, 72, FFP)
    xt, wg, wu, wd = call(
        gather_hidden, 1, (hidden.T, gate_weight, up_weight, down_weight_t), [VM] * 4,
        [(8, 288, 256), wshape, wshape, wshape], [VM, AN, AN, AN], 64, 4,
    )
    full_hidden = xt.reshape(2304, 256).T
    attn_input = row_norm(full_hidden, attn_gain).astype(bf16)
    queries = spin(jnp.dot(attn_input, query_weight, preferred_element_type=f32), cosine, sine).astype(bf16)
    own_proj = jnp.dot(attn_input, kv_weight, preferred_element_type=f32)
    own_part = jnp.where(is_key, spin(own_proj, cosine, sine), own_proj).astype(bf16)
    stay = jnp.where(is_key, own_part[:128], own_part[128:])
    go = jnp.where(is_key, own_part[128:], own_part[:128])
    kv, qa = call(
        exchange_kv, 2, (stay, go, queries), [VM] * 3, [(2, 16, 128, 256), (4, 256, 256)], [VM, VM], 40, 2,
    )
    num, den, page = pl.pallas_call(
        attend,
        out_shape=[jax.ShapeDtypeStruct((4, 256, 256), bf16), jax.ShapeDtypeStruct((4, 8, 256), f32),
                   jax.ShapeDtypeStruct((4, 256, 256), bf16)],
        in_specs=[pl.BlockSpec(memory_space=pltpu.SMEM)] * 3 + [VM] * 2,
        out_specs=[VM] * 3,
        scratch_shapes=[pltpu.VMEM((256, 256), f32), pltpu.VMEM((256, 128), f32)],
        name="attend",
    )(lengths, pair_owner, page_table, qa, kv)
    spot = p.x * 2 + p.yb

    def pick(a, i):
        return lax.dynamic_index_in_dim(a, i, 0, keepdims=False)

    rn, rd, wg, wu, wd = call(
        exchange_partials, 3, (num, den, wg, wu, wd), [VM, VM, AN, AN, AN],
        [(3, 256, 256), jax.ShapeDtypeStruct((3, 8, 256), f32), wshape, wshape, wshape],
        [VM, VM, AN, AN, AN], 20, 0, {2: 2, 3: 3, 4: 4},
    )
    pages = pick(page, spot).astype(f32)
    for o in range(1, 4):
        dx, dy = o // 2, o % 2
        peer = ((p.x + dx) % 2) * 2 + (p.yb + dy) % 2
        pages += lax.ppermute(pick(page, peer), ("seq", "tensor"), quad_route(dx, dy)).astype(f32)
    kv_pages = pages.astype(bf16).reshape(2, 128, 256)
    numerator = pick(num, spot).astype(f32) + rn[0].astype(f32) + rn[1].astype(f32) + rn[2].astype(f32)
    denominator = (pick(den, spot) + rd[0] + rd[1] + rd[2])[0][:, None]
    attended = (numerator / denominator).astype(bf16)
    partial = jnp.dot(attended, out_weight, preferred_element_type=f32).astype(bf16).reshape(2, 4, 32, 2304)
    own_hidden = lax.dynamic_slice_in_dim(full_hidden, p.t * 32, 32, 0)
    mine = pltpu.VMEM((32, 2304), bf16)
    middle, xa, wg, wu, wd = call(
        mix_tensor, 4, (partial, own_hidden, post_gain[None, :], ff_gain[None, :], wg, wu, wd), [VM] * 4 + [AN] * 3,
        [(32, 2304), (4, 4, 32, 2304), wshape, wshape, wshape], [VM, VM, AN, AN, AN], 100, 1,
        {4: 2, 5: 3, 6: 4}, [mine] + reduce_scratch(2),
    )
    rows = xa.reshape(512, 2304)
    gate_val = jnp.dot(rows, wg.reshape(2304, FFP), preferred_element_type=f32)
    up_val = jnp.dot(rows, wu.reshape(2304, FFP), preferred_element_type=f32)
    column = jnp.arange(FFP, dtype=jnp.int32)
    keep = (p.x == 0) | (column >= FFP - FFO)
    inner = jnp.where(keep[None, :], jax.nn.gelu(gate_val, approximate=True) * up_val, 0.0).astype(bf16)
    ff_partial = lax.dot_general(
        inner, wd.reshape(2304, FFP), (((1,), (1,)), ((), ())), preferred_element_type=f32
    ).astype(bf16).reshape(4, 4, 32, 2304)
    (fr,) = call(
        mix_plane, 5, (ff_partial, middle, ff_post_gain[None, :]), [VM] * 3, [(8, 32, 2304)], [VM], 60, 1, None,
        [mine] + reduce_scratch(4),
    )
    final_rows = fr.reshape(256, 2304)
    next_input = row_norm(final_rows, next_gain).astype(bf16)
    hidden_out = lax.dynamic_slice_in_dim(final_rows, p.t * 288, 288, 1)
    next_query = spin(jnp.dot(next_input, next_query_weight, preferred_element_type=f32), cosine, sine).astype(bf16)
    next_proj = jnp.dot(next_input, next_kv_weight, preferred_element_type=f32)
    next_kv = jnp.where(is_key, spin(next_proj, cosine, sine), next_proj).astype(bf16)
    return (hidden_out, next_query, next_kv, kv_pages)


def solution(mesh):
    wide = P("seq", "tensor")
    cols = P(None, "tensor")
    in_specs = (wide, P(), cols, cols, P("tensor", None), P(), P(), P(), wide, wide, wide, P(), cols, cols, P(), P(), P())
    out_specs = (wide, wide, wide, P("seq", None, "tensor"))
    return jax.shard_map(body, mesh=mesh, in_specs=in_specs, out_specs=out_specs, check_vma=False)
```

time: 296 us -> 229 us (0.77); the launches traced: 290 us -> 228 us
  Pallas kernels: 234 us -> 176 us
  other arithmetic: 25.4 us -> 12 us
  starting transfers between devices: 0 us -> 5.04 us
    pallas_call x8 -> x6, Pallas kernels: 234 us -> 176 us  [the longest x5 166 us: call(): pl.pallas_call(body, out_shape=[s if isinstance(s, jax.ShapeDtypeStruct)...]
    ppermute x0 -> x3, starting transfers between devices: none -> 5.04 us  [body(): lax.ppermute(pick(page, peer), ('seq', 'tensor'), quad_route(dx, dy))]
    reduce_sum x7 -> x1, other arithmetic: 6.24 us -> 1.29 us  [body(): jnp.sum(jnp.where(jnp.arange(32, dtype=jnp.int32) == p.s, pair_owner, 0))]
    reduce_sum x5 -> x2, other arithmetic: 6.57 us -> 3.19 us  [row_norm(): jnp.mean(values * values, axis=-1, keepdims=True) + EPS]
  transfers between devices with their start and end apart: 0 -> 3, of which waited for: 0 -> 0; matrix products, arithmetic and copies ran while one was open for 0% -> 13% of each run, Pallas kernels for 0% -> 46%
where the time goes in v2:
time: 229 us; the launch traced here: 228 us
  Pallas kernels  176 us (77%)
  matrix products  23.3 us (10%)
  other arithmetic  12 us (5%)
  local copies, waits for them, and re-layouts  7.78 us (3%)
  starting transfers between devices  5.04 us (2%)
  between operations  4.22 us (2%)
    pallas_call x5, Pallas kernels, call(): pl.pallas_call(body, out_shape=[s if isinstance(s, jax.ShapeDtypeStruct)...  166 us
    dot_general x1, matrix products, body(): lax.dot_general(inner, wd.reshape(2304, FFP), (((1,), (1,)), ((), ())), p...  9.69 us
    pallas_call x1, Pallas kernels, body(): pl.pallas_call(attend, out_shape=[jax.ShapeDtypeStruct((4, 256, 256), bf1...  9.45 us
    ppermute x3, starting transfers between devices, body(): lax.ppermute(pick(page, peer), ('seq', 'tensor'), quad_route(dx, dy))  5.04 us
  transfers between devices with their start and end apart: 3, of which 0 were waited for; matrix products, arithmetic and copies ran while one was open for 13% of the time, Pallas kernels for 46%

profile of v2, /device:TPU:4, one launch (start us, length us, event | category | flops | bytes accessed | tf_op | source)
XLA Modules:
  0.0 228.1 jit_solution(16207738433771335734)
XLA Ops:
  0.8 1.4 fusion.72
  2.1 1.3 fusion.65
  4.7 36.9 %gather_hidden.1 = (bf16[8,288,256]{2,1,0:T(8,128)(2,1)}, bf16[2,16,72,640]{3,2,1,0:T(8,128)(2,1)}, bf16[2,16,72,640]{3,2,1,0:T(8,128)(2,1)}, bf16[2,16,72,640]{3,2,1,0:T(8,128)(2,1)}) custom-call(bf16[288,256]{1,0:T(8,128)(2,1)} %bitcast.52, bf16[72,1152]{1,0:T(8,128)(2,1)} %gate.1, bf16[72,1152]{1,0:T(8,128)(2,1)} %up.1, bf16[72,1152]{1,0:T(8,128)(2,1)} %down.1), custom_call_target="tpu_custom_call" | custom-call | tf_op jit(solution)/shard_map/gather_hidden/pallas_call | solution.py:429
  41.6 1.6 fusion
  45.9 2.7 %fusion.16 = f32[256,256]{1,0:T(8,128)S(1)} fusion(bf16[2304,256]{1,0:T(8,128)(2,1)} %param.20, bf16[2304,256]{1,0:T(8,128)(2,1)} %bitcast.46, f32[2304]{0:T(1024)S(1)} %copy-done.8, f32[256]{0:T(256)S(1)} %add_rsqrt_fusion.1), kind=kOutput, calls=%fused_computation.23 | convolution fusion | flops 304349184 | bytes 2631680 | tf_op jit(solution)/shard_map/dot_general | solution.py:566
  49.9 0.9 fusion.14
  52.1 24.1 %exchange_kv.1 = (bf16[2,16,128,256]{3,2,1,0:T(8,128)(2,1)}, bf16[4,256,256]{2,1,0:T(8,128)(2,1)}) custom-call(bf16[128,256]{1,0:T(8,128)(2,1)} %get-tuple-element.54.stay, bf16[128,256]{1,0:T(8,128)(2,1)} %get-tuple-element.53.go, bf16[256,256]{1,0:T(8,128)(2,1)} %pad_maximum_fusion.q), custom_call_target="tpu_custom_call" | custom-call | tf_op jit(solution)/shard_map/exchange_kv/pallas_call | solution.py:429
  76.1 9.4 %attend.1 = (bf16[4,256,256]{2,1,0:T(8,128)(2,1)}, f32[4,8,256]{2,1,0:T(8,128)}, bf16[4,256,256]{2,1,0:T(8,128)(2,1)}) custom-call(s32[4]{0:T(128)} %lengths.1, s32[32]{0:T(128)} %owner.1, s32[64]{0:T(128)} %table.1, bf16[4,256,256]{2,1,0:T(8,128)(2,1)} %get-tuple-element.24.qa, bf16[2,16,128,256]{3,2,1,0:T(8,128)(2,1)} %get-tuple-element.25.kv), custom_call_target="tpu_custom_call" | custom-call | tf_op jit(solution)/shard_map/attend/pallas_call | solution.py:573
  85.6 1.7 dynamic-slice_bitcast_fusion.2
  87.3 3.6 %collective-permute-start.1 = (bf16[256,256]{1,0:T(8,128)(2,1)S(1)}, bf16[256,256]{1,0:T(8,128)(2,1)}, u32[]{:S(2)}, u32[]{:S(2)}) collective-permute-start(bf16[256,256]{1,0:T(8,128)(2,1)S(1)} %get-tuple-element.44), channel_id=1, source_target_pairs={{0,128},{1,129},{2,130},{3,131},{4,132},{5,133},{6,134},{7,135},{8... | collective-permute-start | bytes 393224 | tf_op jit(solution)/shard_map/ppermute | solution.py:596
  90.9 1.5 collective-permute-start.2
  92.3 23.0 %exchange_partials.1 = (bf16[3,256,256]{2,1,0:T(8,128)(2,1)}, f32[3,8,256]{2,1,0:T(8,128)}, bf16[2,16,72,640]{3,2,1,0:T(8,128)(2,1)}, bf16[2,16,72,640]{3,2,1,0:T(8,128)(2,1)}, bf16[2,16,72,640]{3,2,1,0:T(8,128)(2,1)}) custom-call(bf16[4,256,256]{2,1,0:T(8,128)(2,1)} %get-tuple-element.26.num, ...), custom_call_target="tpu_custom_call", output_to_operand_aliasing={{2}: (2, {}), {3}: (3, {}), {4}: (4, {})} | custom-call | tf_op jit(solution)/shard_map/exchange_partials/pallas_call | solution.py:429
  115.4 0.7 fusion.71
  116.4 0.9 copy.55
  119.8 2.7 %convolution_convert_fusion.1 = bf16[256,2304]{1,0:T(8,128)(2,1)} fusion(bf16[256,2304]{1,0:T(8,128)(2,1)S(1)} %copy-done, f32[256]{0:T(256)S(1)} %bitcast.54, bf16[3,256,256]{2,1,0:T(8,128)(2,1)} %get-tuple-element.31, bf16[4,256,256]{2,1,0:T(8,128)(2,1)} %get-tuple-element.26.num, s32[]{:T(128)S(6)} %select_n.128), kind=kOutput, calls=%fused_computation.1 | convolution fusion | flops 303169536 | bytes 2884612 | tf_op jit(solution)/shard_map/dot_general | solution.py:601
  122.5 43.6 %mix_tensor.1 = (bf16[32,2304]{1,0:T(8,128)(2,1)}, bf16[4,4,32,2304]{3,2,1,0:T(8,128)(2,1)}, bf16[2,16,72,640]{3,2,1,0:T(8,128)(2,1)}, bf16[2,16,72,640]{3,2,1,0:T(8,128)(2,1)}, bf16[2,16,72,640]{3,2,1,0:T(8,128)(2,1)}) custom-call(bf16[2,4,32,2304]{3,2,1,0:T(8,128)(2,1)} %bitcast.50, ...), custom_call_target="tpu_custom_call", output_to_operand_aliasing={{2}: (4, {}), {3}: (5, {}), {4}: (6, {})} | custom-call | tf_op jit(solution)/shard_map/mix_tensor/pallas_call | solution.py:429
  166.1 4.5 %fusion.73 = f32[512,640]{1,0:T(8,128)S(1)} fusion(bf16[512,2304]{1,0:T(8,128)(2,1)} %bitcast.55, bf16[2304,640]{1,0:T(8,128)(2,1)} %bitcast.40), kind=kOutput, calls=%fused_computation.103 | convolution fusion | flops 1509949440 | bytes 6619136 | tf_op jit(solution)/shard_map/dot_general | solution.py:610
  170.6 9.7 %convolution_convert_fusion = bf16[512,2304]{1,0:T(8,128)(2,1)} fusion(bf16[2304,640]{1,0:T(8,128)(2,1)} %bitcast.42, bf16[512,2304]{1,0:T(8,128)(2,1)} %bitcast.56, bf16[2304,640]{1,0:T(8,128)(2,1)} %bitcast.41, f32[512,640]{1,0:T(8,128)S(1)} %fusion.73, pred[640]{0:T(1024)(128)(4,1)S(1)} %fusion.58), kind=kOutput, calls=%fused_computation | convolution fusion | flops 3024683008 | bytes 11928192 | tf_op jit(solution)/shard_map/dot_general | solution.py:615
  180.3 38.7 %mix_plane.1 = bf16[8,32,2304]{2,1,0:T(8,128)(2,1)} custom-call(bf16[4,4,32,2304]{3,2,1,0:T(8,128)(2,1)} %bitcast.49, bf16[32,2304]{1,0:T(8,128)(2,1)} %get-tuple-element.40.mid, f32[1,2304]{1,0:T(1,128)} %broadcast_in_dim.47.gain), custom_call_target="tpu_custom_call" | custom-call | tf_op jit(solution)/shard_map/mix_plane/pallas_call | solution.py:429
  219.0 1.6 multiply_reduce_fusion
  220.7 2.3 %fusion.13 = f32[256,256]{1,0:T(8,128)S(1)} fusion(bf16[2304,256]{1,0:T(8,128)(2,1)} %param.29, bf16[256,2304]{1,0:T(8,128)(2,1)} %bitcast.43, f32[2304]{0:T(1024)S(1)} %copy-done.9, f32[256]{0:T(256)S(1)} %rsqrt.21), kind=kOutput, calls=%fused_computation.21 | convolution fusion | flops 304349184 | bytes 2631680 | tf_op jit(solution)/shard_map/dot_general | solution.py:625
  224.8 0.8 copy.56
  225.6 0.7 fusion.19
  226.3 1.8 fusion.22
  (44 shorter events, 7.9 us)
Async XLA Ops:
  0.6 119.2 %copy-start = (bf16[256,2304]{1,0:T(8,128)(2,1)S(1)}, bf16[256,2304]{1,0:T(8,128)(2,1)}, u32[]{:S(2)}) copy-start(bf16[256,2304]{1,0:T(8,128)(2,1)} %param.21) | copy-start | bytes 3538948
  0.6 45.2 %copy-start.8 = (f32[2304]{0:T(1024)S(1)}, f32[2304]{0:T(1024)}, u32[]{:S(2)}) copy-start(f32[2304]{0:T(1024)} %param.18) | copy-start | bytes 27652
  45.8 4.0 %copy-start.2 = (bf16[8,288,256]{2,1,0:T(8,128)(2,1)S(1)}, bf16[8,288,256]{2,1,0:T(8,128)(2,1)}, u32[]{:S(2)}) copy-start(bf16[8,288,256]{2,1,0:T(8,128)(2,1)} %get-tuple-element.23) | copy-start | bytes 3538948
  45.9 4.0 %copy-start.6 = (bf16[2304,256]{1,0:T(8,128)(2,1)S(1)}, bf16[2304,256]{1,0:T(8,128)(2,1)}, u32[]{:S(2)}) copy-start(bf16[2304,256]{1,0:T(8,128)(2,1)} %param.19) | copy-start | bytes 3538948
  87.3 139.0 %collective-permute-start = (bf16[256,256]{1,0:T(8,128)(2,1)}, bf16[256,256]{1,0:T(8,128)(2,1)S(1)}, u32[]{:S(2)}, u32[]{:S(2)}) collective-permute-start(bf16[256,256]{1,0:T(8,128)(2,1)} %get-tuple-element.42), channel_id=1, source_target_pairs={{0,1},{1,0},{2,3},{3,2},{4,5},{5,4},{6,7},{7,6},{8,9},{9,8},{10,11... | collective-permute-start | bytes 393224 | tf_op jit(solution)/shard_map/ppermute | solution.py:596
  87.3 139.0 %collective-permute-start.1 = (bf16[256,256]{1,0:T(8,128)(2,1)S(1)}, bf16[256,256]{1,0:T(8,128)(2,1)}, u32[]{:S(2)}, u32[]{:S(2)}) collective-permute-start(bf16[256,256]{1,0:T(8,128)(2,1)S(1)} %get-tuple-element.44), channel_id=1, source_target_pairs={{0,128},{1,129},{2,130},{3,131},{4,132},{5,133},{6,134},{7,135},{8... | collective-permute-start | bytes 393224 | tf_op jit(solution)/shard_map/ppermute | solution.py:596
  90.9 135.5 %collective-permute-start.2 = (bf16[256,256]{1,0:T(8,128)(2,1)S(1)}, bf16[256,256]{1,0:T(8,128)(2,1)}, u32[]{:S(2)}, u32[]{:S(2)}) collective-permute-start(bf16[256,256]{1,0:T(8,128)(2,1)S(1)} %get-tuple-element.43), channel_id=1, source_target_pairs={{0,129},{1,128},{2,131},{3,130},{4,133},{5,132},{6,135},{7,134},{8... | collective-permute-start | bytes 393224 | tf_op jit(solution)/shard_map/ppermute | solution.py:596
  115.4 1.9 copy-start.3
  115.4 2.5 %copy-start.4 = (f32[2304]{0:T(1024)S(1)}, f32[2304]{0:T(1024)}, u32[]{:S(2)}) copy-start(f32[2304]{0:T(1024)} %param.23) | copy-start | bytes 27652
  115.4 3.1 %copy-start.5 = (f32[2304]{0:T(1024)S(1)}, f32[2304]{0:T(1024)}, u32[]{:S(2)}) copy-start(f32[2304]{0:T(1024)} %param.24) | copy-start | bytes 27652
  180.3 40.4 %copy-start.9 = (f32[2304]{0:T(1024)S(1)}, f32[2304]{0:T(1024)}, u32[]{:S(2)}) copy-start(f32[2304]{0:T(1024)} %param.28) | copy-start | bytes 27652
  220.6 2.9 %copy-start.1 = (bf16[8,32,2304]{2,1,0:T(8,128)(2,1)S(1)}, bf16[8,32,2304]{2,1,0:T(8,128)(2,1)}, u32[]{:S(2)}) copy-start(bf16[8,32,2304]{2,1,0:T(8,128)(2,1)} %mix_plane.1) | copy-start | bytes 3538948
  220.7 2.9 %copy-start.7 = (bf16[2304,256]{1,0:T(8,128)(2,1)S(1)}, bf16[2304,256]{1,0:T(8,128)(2,1)}, u32[]{:S(2)}) copy-start(bf16[2304,256]{1,0:T(8,128)(2,1)} %param.30) | copy-start | bytes 3538948

commit v3 on v2

--- a/solution.py
+++ b/solution.py
@@ -84,6 +84,7 @@
     def make(self, src, dst, dev):
         i = self.n
         self.n += 1
+        assert i < self.send.shape[0]
         return pltpu.make_async_remote_copy(
             src_ref=src, dst_ref=dst, send_sem=self.send.at[i], recv_sem=self.recv.at[i],
             device_id=dev, device_id_type=MESH,
@@ -107,7 +108,7 @@
     pl.semaphore_wait(sem, len(peers))
 
 
-def gather_grid(p, cps, own, view, nx):
+def gather_grid(p, cps, own, view, nx, middle=lambda: None):
     size = (nx, 4)
 
     def send(h, a, b, sub, dim, sign):
@@ -140,6 +141,7 @@
 
     for h in range(2):
         onward(h, 0)
+    middle()
     for h in range(2):
         if far[h]:
             for cp in far[h]:
@@ -245,34 +247,27 @@
 
 
 def normed(values, gain):
-    return values * lax.rsqrt(jnp.mean(values * values, axis=1, keepdims=True) + EPS) * gain[...]
-
-
-def weight_round(p, cps, ws, d):
+    return values * lax.rsqrt(jnp.mean(values * values, axis=1, keepdims=True) + EPS) * gain[...][None, :]
+
+
+def weight_send(p, cps, ws, own, d):
+    org = p.x if own else 1 - p.x
     got = []
-    right = ((p.z + 9 - d) % 8) * 2 + p.c
-    left = ((p.z + 7 + d) % 8) * 2 + p.c
-    for w in ws:
-        if d < 4:
-            got.append((cps.go(w.at[:, right], w.at[:, right], p.zp()), w))
-            got.append((cps.go(w.at[:, left], w.at[:, left], p.zm()), w))
-        else:
-            got.append((cps.go(w.at[0, right], w.at[0, right], p.zp()), w))
-            got.append((cps.go(w.at[1, left], w.at[1, left], p.zm()), w))
-    return got
-
-
-def weight_finish(p, cps, got, d):
-    right = ((p.z + 8 - d) % 8) * 2 + p.c
-    left = ((p.z + d) % 8) * 2 + p.c
+    for sign, dev in ((-1, p.zp()), (1, p.zm())):
+        if d == 4 and (sign == -1) != own:
+            continue
+        slot = ((p.z + 8 + sign * (d - 1)) % 8) * 2 + p.c
+        got += [(cps.go(w.at[org, slot], w.at[org, slot], dev), w, sign) for w in ws]
+    return org, got, d
+
+
+def weight_take(p, cps, sent):
+    org, got, d = sent
     out = []
-    for i, (cp, w) in enumerate(got):
+    for cp, w, sign in got:
         cp.wait_recv()
-        if d < 4:
-            slot = right if i % 2 == 0 else left
-            out.append(cps.go(w.at[:, slot], w.at[:, slot], p.sib()))
-        elif i % 2 == 1:
-            out.append(cps.go(w.at[:, right], w.at[:, right], p.sib()))
+        slot = ((p.z + 8 + sign * d) % 8) * 2 + p.c
+        out.append(cps.go(w.at[org, slot], w.at[org, slot], p.sib()))
     return out
 
 
@@ -285,10 +280,11 @@
     mine = pl.ds(pl.multiple_of(p.x * FFO, 128), FFP)
     other = pl.ds(pl.multiple_of((1 - p.x) * FFO, 128), FFP)
     swaps = [cps.go(a.at[:, other], w.at[p.x, slot], p.xpart()) for a, w in zip((gate, up, down), ws)]
-    ring = [cps.go(a.at[:, mine], w.at[p.x, slot], dev) for a, w in zip((gate, up, down), ws)
-            for dev in (p.zp(), p.zm())]
+    ring = [(cps.go(a.at[:, mine], w.at[p.x, slot], dev), w, sign)
+            for sign, dev in ((-1, p.zp()), (1, p.zm())) for a, w in zip((gate, up, down), ws)]
     locs = [pltpu.make_async_copy(a.at[:, mine], w.at[p.x, slot], loc.at[i])
             for i, (a, w) in enumerate(zip((gate, up, down), ws))]
+    sib = [cps.go(a.at[:, mine], w.at[p.x, slot], p.sib()) for a, w in zip((gate, up, down), ws)]
 
     def view(dx, dy, h, sub):
         t = ((p.t // 4 + 2 + dx) % 2) * 4 + (p.Y + 4 + dy) % 4
@@ -298,22 +294,20 @@
     locs.append(pltpu.make_async_copy(ht, xt.at[p.t], loc.at[3]))
     for cp in locs:
         cp.start()
-    gather_grid(p, cps, lambda h: ht.at[pl.ds(h * 144, 144)], view, 2)
-    for cp in swaps:
-        cp.wait_recv()
-    for w in ws:
-        ring += [cps.go(w.at[1 - p.x, slot], w.at[1 - p.x, slot], dev) for dev in (p.zp(), p.zm())]
+    swapped = []
+
+    def middle():
+        for cp in swaps:
+            cp.wait_recv()
+        swapped.append(weight_send(p, cps, ws, False, 1))
+        for w in ws:
+            sib.append(cps.go(w.at[1 - p.x, slot], w.at[1 - p.x, slot], p.sib()))
+        sib.extend(weight_take(p, cps, (p.x, ring, 1)))
+
+    gather_grid(p, cps, lambda h: ht.at[pl.ds(h * 144, 144)], view, 2, middle)
+    sib += weight_take(p, cps, swapped[0])
     for cp in locs:
         cp.wait()
-    sib = [cps.go(w.at[:, slot], w.at[:, slot], p.sib()) for w in ws]
-    right = ((p.z + 7) % 8) * 2 + p.c
-    left = ((p.z + 1) % 8) * 2 + p.c
-    for i in range(6):
-        ring[i].wait_recv()
-        ring[i + 6].wait_recv()
-        w = ws[i // 2]
-        at = right if i % 2 == 0 else left
-        sib.append(cps.go(w.at[:, at], w.at[:, at], p.sib()))
     for cp in sib:
         cp.wait_recv()
     cps.drain_sends()
@@ -363,13 +357,12 @@
 
 def exchange_partials(num, den, wg0, wu0, wd0, rn, rd, wg, wu, wd, send, recv):
     p = Place()
-    quads = [p.quad(o) for o in range(1, 4)]
-    barrier([d for _, _, d in quads] + [p.zp(), p.zm(), p.sib()])
+    quads = [p.quad(o)[2] for o in range(1, 4)]
+    barrier(quads + [p.zp(), p.zm(), p.sib()])
     cps = Copies(send, recv)
-    ex = [cps.go(num.at[x * 2 + yb], rn.at[o], d) for o, (x, yb, d) in enumerate(quads)]
-    ex += [cps.go(den.at[x * 2 + yb], rd.at[o], d) for o, (x, yb, d) in enumerate(quads)]
-    got = weight_round(p, cps, (wg, wu, wd), 2)
-    sib = weight_finish(p, cps, got, 2)
+    ex = [cps.go(num.at[o + 1], rn.at[o], d) for o, d in enumerate(quads)]
+    ex += [cps.go(den.at[o + 1], rd.at[o], d) for o, d in enumerate(quads)]
+    sib = weight_take(p, cps, weight_send(p, cps, (wg, wu, wd), True, 2))
     for cp in ex + sib:
         cp.wait_recv()
     cps.drain_sends()
@@ -380,7 +373,7 @@
     barrier(p.around(4) + [p.zp(), p.zm(), p.sib()])
     cps = Copies(send, recv)
     ws = (wg, wu, wd)
-    got = weight_round(p, cps, ws, 3)
+    rest = [weight_send(p, cps, ws, False, 2), weight_send(p, cps, ws, True, 3)]
     bufs, sums = reduce_bufs(scratch)
     total = jnp.concatenate(reduce_grid(p, cps, o_ref, bufs, sums, 2), axis=1)
     middle = (hid[...].astype(f32) + normed(total, post_gain)).astype(bf16)
@@ -388,15 +381,22 @@
     mine[...] = normed(middle.astype(f32), ff_gain).astype(bf16)
     lc = pltpu.make_async_copy(mine, xa.at[p.X, p.Y], loc.at[0])
     lc.start()
-    sib = weight_finish(p, cps, got, 3)
-    got = weight_round(p, cps, ws, 4)
+    sib = weight_take(p, cps, rest[0])
+    rest.append(weight_send(p, cps, ws, False, 3))
+    sib += weight_take(p, cps, rest[1])
+    rest.append(weight_send(p, cps, ws, True, 4))
+
+    def middle_step():
+        sib.extend(weight_take(p, cps, rest[2]))
+        rest.append(weight_send(p, cps, ws, False, 4))
 
     def view(dx, dy, h, sub):
         rows = slice(0, 32) if sub is None else ROW[sub]
         return xa.at[(p.X + 4 + dx) % 4, (p.Y + 4 + dy) % 4, rows, COL[h]]
 
-    gather_grid(p, cps, lambda h: mine.at[:, COL[h]], view, 4)
-    sib += weight_finish(p, cps, got, 4)
+    gather_grid(p, cps, lambda h: mine.at[:, COL[h]], view, 4, middle_step)
+    sib += weight_take(p, cps, rest[3])
+    sib += weight_take(p, cps, rest[4])
     for cp in sib:
         cp.wait_recv()
     lc.wait()
@@ -452,7 +452,10 @@
 
     def key_block(k):
         b = owner[p.x * 16 + k]
-        return jnp.where(p.yb == 0, b, 63 - b)
+        return jnp.where((p.yb + k // 2) % 2 == 0, b, 63 - b)
+
+    def rel(x, h):
+        return ((x + p.x) % 2) * 2 + (h + p.yb) % 2
 
     for qb in range(4):
         x, blk = qb // 2, qb % 2
@@ -489,8 +492,8 @@
         )
         num = acc[...].astype(bf16)
         for h in range(2):
-            out[2 * x + h, rows, :] = num[h * 128:(h + 1) * 128]
-            out_den[2 * x + h, :, blk * 128:(blk + 1) * 128] = total[:, h * 128:(h + 1) * 128]
+            out[rel(x, h), rows, :] = num[h * 128:(h + 1) * 128]
+            out_den[rel(x, h), :, blk * 128:(blk + 1) * 128] = total[:, h * 128:(h + 1) * 128]
 
     base = p.z * 4 + p.c * 2
 
@@ -509,7 +512,80 @@
         at = jnp.maximum(chosen[n], 0)
         for part in range(2):
             picked = jnp.where(chosen[n] >= 0, kv[part, at].astype(f32), 0.0)
-            out_page[(n // 2) * 2 + part, pl.ds((n % 2) * 128, 128), :] = picked.astype(bf16)
+            out_page[rel(n // 2, part), pl.ds((n % 2) * 128, 128), :] = picked.astype(bf16)
+
+
+def project(normal, wq_ref, wk_ref, cosine, sine, yb):
+    dims = (((1,), (0,)), ((), ()))
+    q = lax.dot_general(normal, wq_ref[...], dims, preferred_element_type=f32)
+    k = lax.dot_general(normal, wk_ref[...], dims, preferred_element_type=f32)
+    c, s = cosine[...], sine[...]
+    key = yb == 0
+
+    def spin(v, turn):
+        a, b = v[:, :128], v[:, 128:]
+        both = jnp.concatenate([a * c - b * s, b * c + a * s], axis=1)
+        return both if turn is None else jnp.where(turn, both, v)
+
+    return spin(q, None).astype(bf16), spin(k, key).astype(bf16)
+
+
+def first_layer(xt, gain, wq, wk, cosine, sine, stay, go, q_ref):
+    p = Place()
+    rows = jnp.transpose(xt[...].reshape(2304, 256).astype(f32))
+    q, own = project(normed(rows, gain).astype(bf16), wq, wk, cosine, sine, p.yb)
+    q_ref[...] = q
+    low = (p.yb + p.z) % 2 == 0
+    stay[...] = jnp.where(low, own[:128].astype(f32), own[128:].astype(f32)).astype(bf16)
+    go[...] = jnp.where(low, own[128:].astype(f32), own[:128].astype(f32)).astype(bf16)
+
+
+def next_layer(fr, gain, wq, wk, cosine, sine, ho, q_ref, k_ref):
+    p = Place()
+    rows = fr[...].reshape(256, 2304).astype(f32)
+    q_ref[...], k_ref[...] = project(normed(rows, gain).astype(bf16), wq, wk, cosine, sine, p.yb)
+    begin = p.t * 288
+    tile = pl.multiple_of((begin // 128) * 128, 128)
+    for i in range(8):
+        window = fr[i, :, pl.ds(tile, 384)].astype(f32)
+        moved = pltpu.roll(window, (384 - begin % 128) % 384, 1)
+        ho[i * 32:(i + 1) * 32, :] = moved[:, :288].astype(bf16)
+
+
+def feed_forward(xa, wg, wu, wd, out, vg, vu, vd, sem):
+    p = Place()
+    cps = [pltpu.make_async_copy(w, v, sem.at[i]) for i, (w, v) in enumerate(((wg, vg), (wu, vu), (wd, vd)))]
+    for cp in cps:
+        cp.start()
+    cps[0].wait()
+    cps[1].wait()
+    lane = lax.broadcasted_iota(jnp.int32, (128, FFP), 1)
+    keep = (lane >= FFP - FFO) | (p.x == 0)
+    dims = (((1,), (1,)), ((), ()))
+    for i in range(4):
+        if i == 1:
+            cps[2].wait()
+        x = xa[i].reshape(128, 2304)
+        g = jnp.dot(x, vg[...], preferred_element_type=f32)
+        u = jnp.dot(x, vu[...], preferred_element_type=f32)
+        inner = jnp.where(keep, jax.nn.gelu(g, approximate=True) * u, 0.0).astype(bf16)
+        if i == 0:
+            held = inner
+            continue
+        if i == 1:
+            out[0] = lax.dot_general(held, vd[...], dims, preferred_element_type=f32).astype(bf16).reshape(4, 32, 2304)
+        out[i] = lax.dot_general(inner, vd[...], dims, preferred_element_type=f32).astype(bf16).reshape(4, 32, 2304)
+
+
+def local_call(body, ins, in_specs, outs, scratch=()):
+    return pl.pallas_call(
+        body,
+        out_shape=[jax.ShapeDtypeStruct(s, bf16) for s in outs],
+        in_specs=in_specs,
+        out_specs=[VM] * len(outs),
+        scratch_shapes=list(scratch),
+        name=body.__name__,
+    )(*ins)
 
 
 def quad_route(dx, dy):
@@ -520,24 +596,11 @@
     return route
 
 
-def row_norm(values, gain_vec):
-    values = values.astype(f32)
-    scale_vec = lax.rsqrt(jnp.mean(values * values, axis=-1, keepdims=True) + EPS)
-    return values * scale_vec * gain_vec
-
-
 def starts_of(tags, lengths):
     e0 = lengths[0]
     e1 = e0 + lengths[1]
     e2 = e1 + lengths[2]
     return jnp.where(tags >= e2, e2, jnp.where(tags >= e1, e1, jnp.where(tags >= e0, e0, 0)))
-
-
-def spin(values, cosine, sine):
-    half_dim = values.shape[-1] // 2
-    a = values[:, :half_dim]
-    b = values[:, half_dim:]
-    return jnp.concatenate([a * cosine - b * sine, b * cosine + a * sine], axis=1)
 
 
 def body(
@@ -560,13 +623,10 @@
         gather_hidden, 1, (hidden.T, gate_weight, up_weight, down_weight_t), [VM] * 4,
         [(8, 288, 256), wshape, wshape, wshape], [VM, AN, AN, AN], 64, 4,
     )
-    full_hidden = xt.reshape(2304, 256).T
-    attn_input = row_norm(full_hidden, attn_gain).astype(bf16)
-    queries = spin(jnp.dot(attn_input, query_weight, preferred_element_type=f32), cosine, sine).astype(bf16)
-    own_proj = jnp.dot(attn_input, kv_weight, preferred_element_type=f32)
-    own_part = jnp.where(is_key, spin(own_proj, cosine, sine), own_proj).astype(bf16)
-    stay = jnp.where(is_key, own_part[:128], own_part[128:])
-    go = jnp.where(is_key, own_part[128:], own_part[:128])
+    stay, go, queries = local_call(
+        first_layer, (xt, attn_gain, query_weight, kv_weight, cosine, sine), [VM] * 6,
+        [(128, 256), (128, 256), (256, 256)],
+    )
     kv, qa = call(
         exchange_kv, 2, (stay, go, queries), [VM] * 3, [(2, 16, 128, 256), (4, 256, 256)], [VM, VM], 40, 2,
     )
@@ -579,52 +639,38 @@
         scratch_shapes=[pltpu.VMEM((256, 256), f32), pltpu.VMEM((256, 128), f32)],
         name="attend",
     )(lengths, pair_owner, page_table, qa, kv)
-    spot = p.x * 2 + p.yb
-
-    def pick(a, i):
-        return lax.dynamic_index_in_dim(a, i, 0, keepdims=False)
-
     rn, rd, wg, wu, wd = call(
         exchange_partials, 3, (num, den, wg, wu, wd), [VM, VM, AN, AN, AN],
         [(3, 256, 256), jax.ShapeDtypeStruct((3, 8, 256), f32), wshape, wshape, wshape],
         [VM, VM, AN, AN, AN], 20, 0, {2: 2, 3: 3, 4: 4},
     )
-    pages = pick(page, spot).astype(f32)
+    pages = page[0].astype(f32)
     for o in range(1, 4):
-        dx, dy = o // 2, o % 2
-        peer = ((p.x + dx) % 2) * 2 + (p.yb + dy) % 2
-        pages += lax.ppermute(pick(page, peer), ("seq", "tensor"), quad_route(dx, dy)).astype(f32)
+        pages += lax.ppermute(page[o], ("seq", "tensor"), quad_route(o // 2, o % 2)).astype(f32)
     kv_pages = pages.astype(bf16).reshape(2, 128, 256)
-    numerator = pick(num, spot).astype(f32) + rn[0].astype(f32) + rn[1].astype(f32) + rn[2].astype(f32)
-    denominator = (pick(den, spot) + rd[0] + rd[1] + rd[2])[0][:, None]
+    numerator = num[0].astype(f32) + rn[0].astype(f32) + rn[1].astype(f32) + rn[2].astype(f32)
+    denominator = (den[0] + rd[0] + rd[1] + rd[2])[0][:, None]
     attended = (numerator / denominator).astype(bf16)
     partial = jnp.dot(attended, out_weight, preferred_element_type=f32).astype(bf16).reshape(2, 4, 32, 2304)
-    own_hidden = lax.dynamic_slice_in_dim(full_hidden, p.t * 32, 32, 0)
+    own_hidden = lax.dynamic_slice_in_dim(xt.reshape(2304, 256), p.t * 32, 32, 1).T
     mine = pltpu.VMEM((32, 2304), bf16)
     middle, xa, wg, wu, wd = call(
-        mix_tensor, 4, (partial, own_hidden, post_gain[None, :], ff_gain[None, :], wg, wu, wd), [VM] * 4 + [AN] * 3,
-        [(32, 2304), (4, 4, 32, 2304), wshape, wshape, wshape], [VM, VM, AN, AN, AN], 100, 1,
+        mix_tensor, 4, (partial, own_hidden, post_gain, ff_gain, wg, wu, wd), [VM] * 4 + [AN] * 3,
+        [(32, 2304), (4, 4, 32, 2304), wshape, wshape, wshape], [VM, VM, AN, AN, AN], 104, 1,
         {4: 2, 5: 3, 6: 4}, [mine] + reduce_scratch(2),
     )
-    rows = xa.reshape(512, 2304)
-    gate_val = jnp.dot(rows, wg.reshape(2304, FFP), preferred_element_type=f32)
-    up_val = jnp.dot(rows, wu.reshape(2304, FFP), preferred_element_type=f32)
-    column = jnp.arange(FFP, dtype=jnp.int32)
-    keep = (p.x == 0) | (column >= FFP - FFO)
-    inner = jnp.where(keep[None, :], jax.nn.gelu(gate_val, approximate=True) * up_val, 0.0).astype(bf16)
-    ff_partial = lax.dot_general(
-        inner, wd.reshape(2304, FFP), (((1,), (1,)), ((), ())), preferred_element_type=f32
-    ).astype(bf16).reshape(4, 4, 32, 2304)
+    (ff_partial,) = local_call(
+        feed_forward, (xa, wg.reshape(2304, FFP), wu.reshape(2304, FFP), wd.reshape(2304, FFP)), [VM] + [AN] * 3,
+        [(4, 4, 32, 2304)], [pltpu.VMEM((2304, FFP), bf16)] * 3 + [pltpu.SemaphoreType.DMA((3,))],
+    )
     (fr,) = call(
-        mix_plane, 5, (ff_partial, middle, ff_post_gain[None, :]), [VM] * 3, [(8, 32, 2304)], [VM], 60, 1, None,
+        mix_plane, 5, (ff_partial, middle, ff_post_gain), [VM] * 3, [(8, 32, 2304)], [VM], 60, 1, None,
         [mine] + reduce_scratch(4),
     )
-    final_rows = fr.reshape(256, 2304)
-    next_input = row_norm(final_rows, next_gain).astype(bf16)
-    hidden_out = lax.dynamic_slice_in_dim(final_rows, p.t * 288, 288, 1)
-    next_query = spin(jnp.dot(next_input, next_query_weight, preferred_element_type=f32), cosine, sine).astype(bf16)
-    next_proj = jnp.dot(next_input, next_kv_weight, preferred_element_type=f32)
-    next_kv = jnp.where(is_key, spin(next_proj, cosine, sine), next_proj).astype(bf16)
+    hidden_out, next_query, next_kv = local_call(
+        next_layer, (fr, next_gain, next_query_weight, next_kv_weight, cosine, sine), [VM] * 6,
+        [(256, 288), (256, 256), (256, 256)],
+    )
     return (hidden_out, next_query, next_kv, kv_pages)
 
 

time: 229 us -> 209 us (0.913)
  matrix products: 23.3 us -> 2.64 us
  other arithmetic: 12 us -> 4.93 us
  Pallas kernels: 176 us -> 182 us
    pallas_call x0 -> x3, Pallas kernels: none -> 21.2 us  [local_call(): pl.pallas_call(body, out_shape=[jax.ShapeDtypeStruct(s, bf16) for s in ou...]
    dot_general x6 -> x0, matrix products: 20.7 us -> none  [the longest x1 9.69 us: body(): lax.dot_general(inner, wd.reshape(2304, FFP), (((1,), (1,)), ((), ())), p...]
    pallas_call x5, Pallas kernels: 166 us -> 152 us  [call(): pl.pallas_call(body, out_shape=[s if isinstance(s, jax.ShapeDtypeStruct)...]
    reduce_sum x2 -> x0, other arithmetic: 3.19 us -> none  [row_norm(): jnp.mean(values * values, axis=-1, keepdims=True) + EPS]
  transfers between devices with their start and end apart: 3 -> 3, of which waited for: 0 -> 0; matrix products, arithmetic and copies ran while one was open for 13% -> 3% of each run, Pallas kernels for 46% -> 55%
where the time goes in v3:
time: 209 us; the launch traced here: 206 us
  Pallas kernels  182 us (87%)
  local copies, waits for them, and re-layouts  7.38 us (4%)
  starting transfers between devices  4.99 us (2%)
  other arithmetic  4.93 us (2%)
  between operations  3.98 us (2%)
  matrix products  2.64 us (1%)
    pallas_call x5, Pallas kernels, call(): pl.pallas_call(body, out_shape=[s if isinstance(s, jax.ShapeDtypeStruct)...  152 us
    pallas_call x3, Pallas kernels, local_call(): pl.pallas_call(body, out_shape=[jax.ShapeDtypeStruct(s, bf16) for s in ou...  21.2 us
    pallas_call x1, Pallas kernels, body(): pl.pallas_call(attend, out_shape=[jax.ShapeDtypeStruct((4, 256, 256), bf1...  9.09 us
    ppermute x3, starting transfers between devices, body(): lax.ppermute(page[o], ('seq', 'tensor'), quad_route(o // 2, o % 2))  4.99 us
  transfers between devices with their start and end apart: 3, of which 0 were waited for; matrix products, arithmetic and copies ran while one was open for 3% of the time, Pallas kernels for 55%

profile of v3, /device:TPU:4, one launch (start us, length us, event | category | flops | bytes accessed | tf_op | source)
XLA Modules:
  0.0 205.8 jit_solution(12065030300947019896)
XLA Ops:
  0.6 0.0 copy-start
  0.7 1.4 fusion.12
  3.4 1.4 fusion.14
  6.7 0.7 fusion.11
  7.3 1.2 multiply_sine_fusion
  8.6 30.6 %gather_hidden.1 = (bf16[8,288,256]{2,1,0:T(8,128)(2,1)}, bf16[2,16,72,640]{3,2,1,0:T(8,128)(2,1)}, bf16[2,16,72,640]{3,2,1,0:T(8,128)(2,1)}, bf16[2,16,72,640]{3,2,1,0:T(8,128)(2,1)}) custom-call(bf16[288,256]{1,0:T(8,128)(2,1)} %bitcast.33, bf16[72,1152]{1,0:T(8,128)(2,1)} %gate.1, bf16[72,1152]{1,0:T(8,128)(2,1)} %up.1, bf16[72,1152]{1,0:T(8,128)(2,1)} %down.1), custom_call_target="tpu_custom_call" | custom-call | tf_op jit(solution)/shard_map/gather_hidden/pallas_call | solution.py:429
  39.2 4.0 %first_layer.1 = (bf16[128,256]{1,0:T(8,128)(2,1)}, bf16[128,256]{1,0:T(8,128)(2,1)}, bf16[256,256]{1,0:T(8,128)(2,1)}) custom-call(bf16[8,288,256]{2,1,0:T(8,128)(2,1)} %get-tuple-element.29.xt, f32[2304]{0:T(1024)} %gain.3, bf16[2304,256]{1,0:T(8,128)(2,1)} %wq.2, bf16[2304,256]{1,0:T(8,128)(2,1)} %wk.2, f32[256,128]{1,0:T(8,128)} %get-tuple-element.69.cosine, ...), custom_call_target="tpu_custom_call" | custom-call | tf_op jit(solution)/shard_map/first_layer/pallas_call | solution.py:581
  43.2 24.6 %exchange_kv.1 = (bf16[2,16,128,256]{3,2,1,0:T(8,128)(2,1)}, bf16[4,256,256]{2,1,0:T(8,128)(2,1)}) custom-call(bf16[128,256]{1,0:T(8,128)(2,1)} %get-tuple-element.30.stay, bf16[128,256]{1,0:T(8,128)(2,1)} %get-tuple-element.31.go, bf16[256,256]{1,0:T(8,128)(2,1)} %get-tuple-element.32.q), custom_call_target="tpu_custom_call" | custom-call | tf_op jit(solution)/shard_map/exchange_kv/pallas_call | solution.py:429
  67.8 9.1 %attend.1 = (bf16[4,256,256]{2,1,0:T(8,128)(2,1)}, f32[4,8,256]{2,1,0:T(8,128)}, bf16[4,256,256]{2,1,0:T(8,128)(2,1)}) custom-call(s32[4]{0:T(128)} %lengths.1, s32[32]{0:T(128)} %owner.1, s32[64]{0:T(128)} %table.1, bf16[4,256,256]{2,1,0:T(8,128)(2,1)} %get-tuple-element.33.qa, bf16[2,16,128,256]{3,2,1,0:T(8,128)(2,1)} %get-tuple-element.34.kv), custom_call_target="tpu_custom_call" | custom-call | tf_op jit(solution)/shard_map/attend/pallas_call | solution.py:633
  76.9 1.8 slice_bitcast_fusion.2
  78.7 2.1 %collective-permute-start.2 = (bf16[256,256]{1,0:T(8,128)(2,1)}, bf16[256,256]{1,0:T(8,128)(2,1)S(1)}, u32[]{:S(2)}, u32[]{:S(2)}) collective-permute-start(bf16[256,256]{1,0:T(8,128)(2,1)} %get-tuple-element.63), channel_id=1, source_target_pairs={{0,129},{1,128},{2,131},{3,130},{4,133},{5,132},{6,135},{7,134},{8... | collective-permute-start | bytes 393224 | tf_op jit(solution)/shard_map/ppermute | solution.py:649
  80.8 2.9 %collective-permute-start.1 = (bf16[256,256]{1,0:T(8,128)(2,1)S(1)}, bf16[256,256]{1,0:T(8,128)(2,1)S(1)}, u32[]{:S(2)}, u32[]{:S(2)}) collective-permute-start(bf16[256,256]{1,0:T(8,128)(2,1)S(1)} %get-tuple-element.64), channel_id=1, source_target_pairs={{0,128},{1,129},{2,130},{3,131},{4,132},{5,133},{6,134},{7,135},{8... | collective-permute-start | bytes 393224 | tf_op jit(solution)/shard_map/ppermute | solution.py:649
  83.7 0.7 slice.56
  84.4 16.2 %exchange_partials.1 = (bf16[3,256,256]{2,1,0:T(8,128)(2,1)}, f32[3,8,256]{2,1,0:T(8,128)}, bf16[2,16,72,640]{3,2,1,0:T(8,128)(2,1)}, bf16[2,16,72,640]{3,2,1,0:T(8,128)(2,1)}, bf16[2,16,72,640]{3,2,1,0:T(8,128)(2,1)}) custom-call(bf16[4,256,256]{2,1,0:T(8,128)(2,1)} %get-tuple-element.35.num, ...), custom_call_target="tpu_custom_call", output_to_operand_aliasing={{2}: (2, {}), {3}: (3, {}), {4}: (4, {})} | custom-call | tf_op jit(solution)/shard_map/exchange_partials/pallas_call | solution.py:429
  100.6 0.7 fusion.13
  101.3 0.2 constant_dynamic-slice_fusion
  101.6 2.6 %convolution_convert_fusion = bf16[256,2304]{1,0:T(8,128)(2,1)} fusion(bf16[256,2304]{1,0:T(8,128)(2,1)S(1)} %copy-done, f32[256]{0:T(256)S(1)} %bitcast.35, bf16[3,256,256]{2,1,0:T(8,128)(2,1)} %get-tuple-element.40, bf16[4,256,256]{2,1,0:T(8,128)(2,1)} %get-tuple-element.35.num), kind=kOutput, calls=%fused_computation | convolution fusion | flops 303169536 | bytes 2884608 | tf_op jit(solution)/shard_map/dot_general | solution.py:654
  104.2 0.9 copy.31
  105.1 43.4 %mix_tensor.1 = (bf16[32,2304]{1,0:T(8,128)(2,1)}, bf16[4,4,32,2304]{3,2,1,0:T(8,128)(2,1)}, bf16[2,16,72,640]{3,2,1,0:T(8,128)(2,1)}, bf16[2,16,72,640]{3,2,1,0:T(8,128)(2,1)}, bf16[2,16,72,640]{3,2,1,0:T(8,128)(2,1)}) custom-call(bf16[2,4,32,2304]{3,2,1,0:T(8,128)(2,1)} %bitcast.31, ...), custom_call_target="tpu_custom_call", output_to_operand_aliasing={{2}: (4, {}), {3}: (5, {}), {4}: (6, {})} | custom-call | tf_op jit(solution)/shard_map/mix_tensor/pallas_call | solution.py:429
  148.6 13.3 %feed_forward.1.y_ref = bf16[4,4,32,2304]{3,2,1,0:T(8,128)(2,1)} custom-call(bf16[4,4,32,2304]{3,2,1,0:T(8,128)(2,1)} %get-tuple-element.45.xa, bf16[2304,640]{1,0:T(8,128)(2,1)} %bitcast.27, bf16[2304,640]{1,0:T(8,128)(2,1)} %bitcast.28, bf16[2304,640]{1,0:T(8,128)(2,1)} %bitcast.29), custom_call_target="tpu_custom_call" | custom-call | tf_op jit(solution)/shard_map/feed_forward/pallas_call | solution.py:581
  161.9 36.7 %mix_plane.1.fr = bf16[8,32,2304]{2,1,0:T(8,128)(2,1)} custom-call(bf16[4,4,32,2304]{3,2,1,0:T(8,128)(2,1)} %feed_forward.1.y_ref, bf16[32,2304]{1,0:T(8,128)(2,1)} %get-tuple-element.49.mid, f32[2304]{0:T(1024)} %gain.4), custom_call_target="tpu_custom_call" | custom-call | tf_op jit(solution)/shard_map/mix_plane/pallas_call | solution.py:429
  198.6 3.8 %next_layer.1 = (bf16[256,288]{1,0:T(8,128)(2,1)}, bf16[256,256]{1,0:T(8,128)(2,1)}, bf16[256,256]{1,0:T(8,128)(2,1)}) custom-call(bf16[8,32,2304]{2,1,0:T(8,128)(2,1)} %mix_plane.1.fr, f32[2304]{0:T(1024)} %gain.5, bf16[2304,256]{1,0:T(8,128)(2,1)} %wq.3, bf16[2304,256]{1,0:T(8,128)(2,1)} %wk.3, f32[256,128]{1,0:T(8,128)} %get-tuple-element.69.cosine, ...), custom_call_target="tpu_custom_call" | custom-call | tf_op jit(solution)/shard_map/next_layer/pallas_call | solution.py:581
  202.5 1.7 copy.30
  204.2 1.6 fusion.2
  (9 shorter events, 0.0 us)
Async XLA Ops:
  0.6 101.0 %copy-start = (bf16[256,2304]{1,0:T(8,128)(2,1)S(1)}, bf16[256,2304]{1,0:T(8,128)(2,1)}, u32[]{:S(2)}) copy-start(bf16[256,2304]{1,0:T(8,128)(2,1)} %param.21) | copy-start | bytes 3538948
  78.7 125.5 %collective-permute-start = (bf16[256,256]{1,0:T(8,128)(2,1)}, bf16[256,256]{1,0:T(8,128)(2,1)S(1)}, u32[]{:S(2)}, u32[]{:S(2)}) collective-permute-start(bf16[256,256]{1,0:T(8,128)(2,1)} %get-tuple-element.62), channel_id=1, source_target_pairs={{0,1},{1,0},{2,3},{3,2},{4,5},{5,4},{6,7},{7,6},{8,9},{9,8},{10,11... | collective-permute-start | bytes 393224 | tf_op jit(solution)/shard_map/ppermute | solution.py:649
  78.7 125.5 %collective-permute-start.2 = (bf16[256,256]{1,0:T(8,128)(2,1)}, bf16[256,256]{1,0:T(8,128)(2,1)S(1)}, u32[]{:S(2)}, u32[]{:S(2)}) collective-permute-start(bf16[256,256]{1,0:T(8,128)(2,1)} %get-tuple-element.63), channel_id=1, source_target_pairs={{0,129},{1,128},{2,131},{3,130},{4,133},{5,132},{6,135},{7,134},{8... | collective-permute-start | bytes 393224 | tf_op jit(solution)/shard_map/ppermute | solution.py:649
  80.8 123.4 %collective-permute-start.1 = (bf16[256,256]{1,0:T(8,128)(2,1)S(1)}, bf16[256,256]{1,0:T(8,128)(2,1)S(1)}, u32[]{:S(2)}, u32[]{:S(2)}) collective-permute-start(bf16[256,256]{1,0:T(8,128)(2,1)S(1)} %get-tuple-element.64), channel_id=1, source_target_pairs={{0,128},{1,129},{2,130},{3,131},{4,132},{5,133},{6,134},{7,135},{8... | collective-permute-start | bytes 393224 | tf_op jit(solution)/shard_map/ppermute | solution.py:649
  84.4 17.0 %copy-start.1 = (bf16[8,288,256]{2,1,0:T(8,128)(2,1)S(1)}, bf16[8,288,256]{2,1,0:T(8,128)(2,1)}, u32[]{:S(2)}) copy-start(bf16[8,288,256]{2,1,0:T(8,128)(2,1)} %get-tuple-element.29.xt) | copy-start | bytes 3538948

commit v4 on v3

v4 whole, which is shorter than its diff:
```python
import jax
import jax.numpy as jnp
from jax import lax
from jax.experimental import pallas as pl
from jax.experimental.pallas import tpu as pltpu
import numpy as np
from jax.sharding import PartitionSpec as P

EPS = 1e-06
SOFT_CAP = 50.0
MESH = pl.DeviceIdType.MESH
VM = pl.BlockSpec(memory_space=pltpu.VMEM)
AN = pl.BlockSpec(memory_space=pl.ANY)
FFP = 640
FFO = 512
bf16 = jnp.bfloat16
f32 = jnp.float32


class Place:
    def __init__(self):
        self.s = lax.axis_index("seq")
        self.t = lax.axis_index("tensor")
        self.x = self.s // 16
        self.z = (self.s // 2) % 8
        self.c = self.s % 2
        self.yb = self.t % 2
        self.X = self.x * 2 + self.t // 4
        self.Y = self.t % 4

    def grid(self, X, Y):
        return self.dev(self.seq(X // 2, self.z, self.c), (X % 2) * 4 + Y)

    def near(self, dim, sign, nx):
        if dim == 1:
            return self.grid(self.X, (self.Y + 4 + sign) % 4)
        if nx == 2:
            return self.dev(self.s, (self.t + 4) % 8)
        return self.grid((self.X + 4 + sign) % 4, self.Y)

    def around(self, nx):
        out = [self.near(1, 1, nx), self.near(1, -1, nx), self.near(0, 1, nx)]
        return out + ([self.near(0, -1, nx)] if nx == 4 else [])

    def seq(self, x, z, c):
        return x * 16 + z * 2 + c

    def dev(self, s, t):
        return {"seq": s, "tensor": t}

    def zp(self):
        return self.dev(self.seq(self.x, (self.z + 1) % 8, self.c), self.t)

    def zm(self):
        return self.dev(self.seq(self.x, (self.z + 7) % 8, self.c), self.t)

    def sib(self):
        return self.dev(self.seq(self.x, self.z, 1 - self.c), self.t)

    def xpart(self):
        return self.dev(self.seq(1 - self.x, self.z, self.c), self.t)

    def quad(self, o):
        dx, dy = o // 2, o % 2
        x = (self.x + dx) % 2
        yb = (self.yb + dy) % 2
        return x, yb, self.dev(self.seq(x, self.z, self.c), self.t - self.yb + yb)

    def tens(self, o):
        t = (self.t + o) % 8
        return t, self.dev(self.s, t)

    def plane(self, o):
        j = (self.x * 8 + self.t + o) % 16
        x, t = j // 8, j % 8
        return j, self.dev(self.seq(x, self.z, self.c), t)


class Copies:
    def __init__(self, send, recv):
        self.send, self.recv, self.n, self.live = send, recv, 0, []

    def make(self, src, dst, dev):
        i = self.n
        self.n += 1
        assert i < self.send.shape[0]
        return pltpu.make_async_remote_copy(
            src_ref=src, dst_ref=dst, send_sem=self.send.at[i], recv_sem=self.recv.at[i],
            device_id=dev, device_id_type=MESH,
        )

    def go(self, src, dst, dev):
        cp = self.make(src, dst, dev)
        cp.start()
        self.live.append(cp)
        return cp

    def drain_sends(self):
        for cp in self.live:
            cp.wait_send()


def barrier(peers):
    sem = pltpu.get_barrier_semaphore()
    for dev in peers:
        pl.semaphore_signal(sem, inc=1, device_id=dev, device_id_type=MESH)
    pl.semaphore_wait(sem, len(peers))


def gather_grid(p, cps, own, view, nx, middle=lambda: None):
    size = (nx, 4)

    def send(h, a, b, sub, dim, sign):
        dx, dy = (a, b) if h == 0 else (b, a)
        dst = view(dx, dy, h, sub)
        return cps.go(own(h) if (a, b) == (0, 0) else dst, dst, p.near(dim, sign, nx))

    def spread(h, a, b, dim):
        return [send(h, a, b, None, dim, sign) for sign in ((1, -1) if size[dim] == 4 else (1,))]

    first = [spread(h, 0, 0, h) for h in range(2)]
    second = [{0: spread(h, 0, 0, 1 - h)} for h in range(2)]
    far = [[], []]
    last = []
    for i in range(2):
        for h in range(2):
            if i < len(first[h]):
                first[h][i].wait_recv()
                a = (-1, 1)[i]
                if size[h] == 4:
                    far[h].append(send(h, a, 0, i, h, -a))
                second[h][a] = spread(h, a, 0, 1 - h)

    def onward(h, a):
        for i, cp in enumerate(second[h][a]):
            cp.wait_recv()
            if size[1 - h] == 4:
                b = (-1, 1)[i]
                last.append(send(h, a, b, i, 1 - h, -b))

    for h in range(2):
        onward(h, 0)
    middle()
    for h in range(2):
        if far[h]:
            for cp in far[h]:
                cp.wait_recv()
            second[h][2] = spread(h, 2, 0, 1 - h)
    for a in (-1, 1, 2):
        for h in range(2):
            if a in second[h]:
                onward(h, a)
    for cp in last:
        cp.wait_recv()


ROW = (slice(0, 16), slice(16, 32))
COL = (slice(0, 1152), slice(1152, 2304))


def reduce_line(p, cps, read, view, buf, dim, nx):
    size = (nx, 4)[dim]
    rp, rm, up, dn, bu, bd = buf
    plus, minus = p.near(dim, 1, nx), p.near(dim, -1, nx)
    if size == 2:
        cp = cps.go(view(1, None), rp, plus)

        def finish():
            cp.wait_recv()
            return read(0, None) + rp[...].astype(f32)

        return [finish]
    far0 = cps.go(view(2, 0), up, plus)
    far1 = cps.go(view(2, 1), dn, minus)
    near = [cps.go(view(1, 1), rp.at[:, ROW[1]], plus), cps.go(view(-1, 0), rm.at[:, ROW[0]], minus)]

    def relay():
        far0.wait_recv()
        bu[...] = (read(1, 0) + up[...].astype(f32)).astype(bf16)
        near.append(cps.go(bu, rp.at[:, ROW[0]], plus))
        far1.wait_recv()
        bd[...] = (read(-1, 1) + dn[...].astype(f32)).astype(bf16)
        near.append(cps.go(bd, rm.at[:, ROW[1]], minus))

    def finish():
        for cp in near:
            cp.wait_recv()
        return read(0, None) + rp[...].astype(f32) + rm[...].astype(f32)

    return [relay, finish]


def reduce_grid(p, cps, part, bufs, sums, nx):
    at = (p.X if nx == 4 else p.X % 2, p.Y)
    size = (nx, 4)

    def one(h):
        def view(d, sub):
            rows = slice(0, 32) if sub is None else ROW[sub]
            i = (at[1 - h] + size[1 - h] + d) % size[1 - h]
            return part.at[:, i, rows, COL[h]] if h == 0 else part.at[i, :, rows, COL[h]]

        def read(d, sub):
            return view(d, sub)[...].astype(f32)

        return reduce_line(p, cps, read, view, bufs[h][:6], 1 - h, nx)

    def two(h):
        def view(d, sub):
            rows = slice(0, 32) if sub is None else ROW[sub]
            i = (at[h] + size[h] + d) % size[h]
            return sums[h].at[pl.ds(i, 1), rows]

        def read(d, sub):
            return view(d, sub)[...].astype(f32)

        return reduce_line(p, cps, read, view, bufs[h][6:], h, nx)

    steps = [one(h) for h in range(2)]
    for h in range(2):
        if len(steps[h]) == 2:
            steps[h][0]()
    later = []
    for h in range(2):
        sums[h][...] = steps[h][-1]().astype(bf16)
        later.append(two(h))
    for h in range(2):
        if len(later[h]) == 2:
            later[h][0]()
    return [later[h][-1]()[0] for h in range(2)]


def reduce_scratch(nx):
    out = []
    for h in range(2):
        size = (nx, 4)
        for n, m in ((size[h], size[1 - h]), (1, size[h])):
            del m
            out += [pltpu.VMEM((n, 32, 1152), bf16)] * 2 + [pltpu.VMEM((n, 16, 1152), bf16)] * 4
        out.append(pltpu.VMEM((size[h], 32, 1152), bf16))
    return out


def reduce_bufs(refs):
    return [refs[0:12], refs[13:25]], [refs[12], refs[25]]


def normed(values, gain):
    return values * lax.rsqrt(jnp.mean(values * values, axis=1, keepdims=True) + EPS) * gain[...][None, :]


def weight_send(p, cps, ws, own, d):
    org = p.x if own else 1 - p.x
    got = []
    for sign, dev in ((-1, p.zp()), (1, p.zm())):
        if d == 4 and (sign == -1) != own:
            continue
        slot = ((p.z + 8 + sign * (d - 1)) % 8) * 2 + p.c
        got += [(cps.go(w.at[org, slot], w.at[org, slot], dev), w, sign) for w in ws]
    return org, got, d


def weight_take(p, cps, sent):
    org, got, d = sent
    out = []
    for cp, w, sign in got:
        cp.wait_recv()
        slot = ((p.z + 8 + sign * d) % 8) * 2 + p.c
        out.append(cps.go(w.at[org, slot], w.at[org, slot], p.sib()))
    return out


FREQ = (10000.0 ** (-np.arange(128, dtype=np.float64) / 128)).astype(np.float32)[None, :]


def starts_of(tags, e0, e1, e2):
    return jnp.where(tags >= e2, e2, jnp.where(tags >= e1, e1, jnp.where(tags >= e0, e0, 0)))


def attention_part(
    lengths, owner, table, ht, gate, up, down, freq, attn_gain, wq, wk, wo, post_gain, ff_gain,
    mid, xa, wg, wu, wd, page_out, cosine, sine,
    send, recv, loc, xt, rows_ref, stay, go, q_ref, kv, qa, start_ref, acc, den, num, dn, pg, rn, rd, rp, part, mine,
    *scratch,
):
    p = Place()
    quads = [p.quad(o) for o in range(1, 4)]
    barrier(p.around(4) + [d for _, _, d in quads[1:]] + [p.zp(), p.zm(), p.sib()])
    cps = Copies(send, recv)
    ws = (wg, wu, wd)
    slot = p.z * 2 + p.c

    columns = pl.ds(pl.multiple_of(p.x * FFO, 128), FFP)
    other = pl.ds(pl.multiple_of((1 - p.x) * FFO, 128), FFP)
    swaps = [cps.go(a.at[:, other], w.at[p.x, slot], p.xpart()) for a, w in zip((gate, up, down), ws)]
    ring = [(cps.go(a.at[:, columns], w.at[p.x, slot], dev), w, sign)
            for sign, dev in ((-1, p.zp()), (1, p.zm())) for a, w in zip((gate, up, down), ws)]
    locs = [pltpu.make_async_copy(a.at[:, columns], w.at[p.x, slot], loc.at[i])
            for i, (a, w) in enumerate(zip((gate, up, down), ws))]
    locs.append(pltpu.make_async_copy(ht, xt.at[p.t], loc.at[3]))
    sib = [cps.go(a.at[:, columns], w.at[p.x, slot], p.sib()) for a, w in zip((gate, up, down), ws)]
    for cp in locs:
        cp.start()

    e0 = lengths[0]
    e1 = e0 + lengths[1]
    e2 = e1 + lengths[2]
    row = lax.broadcasted_iota(jnp.int32, (128, 128), 0)
    lane = lax.broadcasted_iota(jnp.int32, (128, 128), 1)
    mypair = owner[p.s]
    for blk in range(2):
        tag = (mypair if blk == 0 else 63 - mypair) * 128 + row
        angle = (tag - starts_of(tag, e0, e1, e2)).astype(f32) * freq[...]
        cosine[blk * 128:(blk + 1) * 128, :] = jnp.cos(angle)
        sine[blk * 128:(blk + 1) * 128, :] = jnp.sin(angle)
    q_blocks = []
    for x in range(2):
        b = owner[x * 16 + p.z * 2 + p.c]
        q_blocks += [b, 63 - b]
    for n in range(4):
        start = starts_of(q_blocks[n] * 128 + row, e0, e1, e2)
        start_ref[n, 0:128, :] = start
        start_ref[n, 128:256, :] = start

    def view_hidden(dx, dy, h, sub):
        t = ((p.t // 4 + 2 + dx) % 2) * 4 + (p.Y + 4 + dy) % 4
        low, n = ((0, 144) if sub is None else ((0, 80), (80, 64))[sub])
        return xt.at[t, pl.ds(h * 144 + low, n)]

    swapped = []

    def middle():
        for cp in swaps:
            cp.wait_recv()
        swapped.append(weight_send(p, cps, ws, False, 1))
        for w in ws:
            sib.append(cps.go(w.at[1 - p.x, slot], w.at[1 - p.x, slot], p.sib()))

    gather_grid(p, cps, lambda h: ht.at[pl.ds(h * 144, 144)], view_hidden, 2, middle)
    locs[3].wait()

    rows = jnp.transpose(xt[...].reshape(2304, 256).astype(f32))
    rows_ref[...] = rows.astype(bf16).reshape(8, 32, 2304)
    normal = normed(rows, attn_gain).astype(bf16)
    own = turned(jnp.dot(normal, wk[...], preferred_element_type=f32), cosine, sine, p.yb == 0)
    low = (p.yb + p.z) % 2 == 0
    stay[...] = jnp.where(low, own[:128], own[128:]).astype(bf16)
    go[...] = jnp.where(low, own[128:], own[:128]).astype(bf16)
    ends = ((7, p.zp()), (1, p.zm()), (0, p.sib()))
    pair = cps.go(go, kv.at[p.yb, 0, p.c], quads[0][2])
    first = [cps.go(stay, kv.at[p.yb, r, p.c], dev) for r, dev in ends]
    got, shared = [first[:2]], [first[2:]]
    lq = [pltpu.make_async_copy(stay, kv.at[p.yb, 0, p.c], loc.at[4])]
    lq[0].start()
    query = turned(jnp.dot(normal, wq[...], preferred_element_type=f32), cosine, sine, None)
    q_ref[...] = query.astype(bf16).reshape(2, 128, 256)
    lq.append(pltpu.make_async_copy(q_ref, qa.at[p.x, p.yb], loc.at[5]))
    lq[1].start()
    pair.wait_recv()
    mate = kv.at[1 - p.yb, 0, p.c]
    first = [cps.go(mate, kv.at[1 - p.yb, r, p.c], dev) for r, dev in ends]
    got.append(first[:2])
    shared[0] += first[2:]
    qs = [cps.go(q_ref, qa.at[p.x, p.yb], d) for _, _, d in quads]
    acc[...] = jnp.zeros_like(acc)
    den[...] = jnp.zeros_like(den)
    for cp in lq:
        cp.wait()
    for cp in qs:
        cp.wait_recv()

    def key_block(z, c):
        b = owner[p.x * 16 + z * 2 + c]
        return jnp.where((p.yb + z) % 2 == 0, b, 63 - b)

    def attend(rel):
        z = (p.z + rel) % 8
        blocks = [key_block(z, c) for c in range(2)]
        keys = kv[0, rel].reshape(256, 256)
        values = kv[1, rel].reshape(256, 256)

        def tile(n, carry):
            b = owner[(n // 2) * 16 + p.z * 2 + p.c]
            q_block = jnp.where(n % 2 == 0, b, 63 - b)
            qt = jnp.concatenate([qa[n // 2, h, n % 2] for h in range(2)], axis=0)
            score = lax.dot_general(qt, keys, (((1,), (1,)), ((), ())), preferred_element_type=f32)
            weight = jnp.exp(SOFT_CAP * jnp.tanh(score * (0.0625 / SOFT_CAP)))
            start = start_ref[n]
            r = lax.broadcasted_iota(jnp.int32, (256, 128), 0) % 128
            l = lax.broadcasted_iota(jnp.int32, (256, 128), 1)
            rounded = []
            for c in range(2):
                kt = blocks[c] * 128 + l
                ok = (kt <= q_block * 128 + r) & (kt >= start)
                rounded.append(jnp.where(ok, weight[:, c * 128:(c + 1) * 128], 0.0).astype(bf16))
            den[n] += rounded[0].astype(f32) + rounded[1].astype(f32)
            acc[n] += jnp.dot(jnp.concatenate(rounded, axis=1), values, preferred_element_type=f32)
            return carry

        lax.fori_loop(0, 4, tile, 0)

    spots = [[0]]
    for d in range(1, 5):
        nxt = [[], []]
        now = []
        for i, kind in enumerate((p.yb, 1 - p.yb)):
            for side, cp in enumerate(got[i]):
                cp.wait_recv()
                rel = 8 - d if side == 0 else d
                here = kv.at[kind, rel, p.c]
                if d < 3 or (d == 3 and side == i):
                    further = kv.at[kind, rel - 1 if side == 0 else rel + 1, p.c]
                    nxt[i].append(cps.go(here, further, (p.zp(), p.zm())[side]))
                now.append(cps.go(here, here, p.sib()))
        got = nxt
        if d == 4:
            sib += weight_take(p, cps, (p.x, ring, 1))
            sib += weight_take(p, cps, swapped[0])
            rest = [weight_send(p, cps, ws, True, 2), weight_send(p, cps, ws, False, 2)]
        for cp in shared[d - 1]:
            cp.wait_recv()
        for rel in spots[d - 1]:
            attend(rel)
        shared.append(now)
        spots.append([8 - d, d] if d < 4 else [4])
    for cp in shared[4]:
        cp.wait_recv()
    attend(4)

    for n in range(4):
        below = lax.dot_general(
            jnp.ones((8, 128), f32), den[n], (((1,), (1,)), ((), ())),
            precision=lax.Precision.HIGHEST, preferred_element_type=f32,
        )
        for h in range(2):
            num[n // 2, h, n % 2] = acc[n, h * 128:(h + 1) * 128, :].astype(bf16)
            dn[n // 2, h, n % 2] = below[:, h * 128:(h + 1) * 128]
    ex = [cps.go(num.at[x, yb], rn.at[o], d) for o, (x, yb, d) in enumerate(quads)]
    ex += [cps.go(dn.at[x, yb], rd.at[o], d) for o, (x, yb, d) in enumerate(quads)]
    base = p.z * 4 + p.c * 2

    def look(i, found):
        page = table[i]
        return tuple(jnp.where(page == (n // 2) * 32 + base + n % 2, i, f) for n, f in enumerate(found))

    wanted = lax.fori_loop(0, 64, look, (jnp.int32(0),) * 4)

    def choose(n, carry):
        want = jnp.where(n == 0, wanted[0], jnp.where(n == 1, wanted[1], jnp.where(n == 2, wanted[2], wanted[3])))
        sums = [jnp.zeros((128, 256), f32)] * 2
        for rel in range(8):
            for c in range(2):
                take = jnp.where(key_block((p.z + rel) % 8, c) == want, 1.0, 0.0)
                sums = [a + kv[kind, rel, c].astype(f32) * take for kind, a in enumerate(sums)]
        for kind in range(2):
            pg[n // 2, kind, n % 2] = sums[kind].astype(bf16)
        return carry

    lax.fori_loop(0, 4, choose, 0)
    px = [cps.go(pg.at[x, yb], rp.at[o], d) for o, (x, yb, d) in enumerate(quads)]
    for cp in ex:
        cp.wait_recv()
    total = num[p.x, p.yb].astype(f32)
    below = dn[p.x, p.yb]
    for o in range(3):
        total += rn[o].astype(f32)
        below += rd[o]
    pieces = []
    for blk in range(2):
        inverse = jnp.transpose(jnp.broadcast_to(1.0 / below[blk, 0:1, :], (128, 128)))
        pieces.append((total[blk] * jnp.concatenate([inverse, inverse], axis=1)).astype(bf16))
    attended = jnp.concatenate(pieces, axis=0)
    part[...] = jnp.dot(attended, wo[...], preferred_element_type=f32).astype(bf16).reshape(2, 4, 32, 2304)
    sib += weight_take(p, cps, rest[0])
    sib += weight_take(p, cps, rest[1])
    rest = [weight_send(p, cps, ws, True, 3), weight_send(p, cps, ws, False, 3)]

    bufs, sums = reduce_bufs(scratch)
    total = jnp.concatenate(reduce_grid(p, cps, part, bufs, sums, 2), axis=1)
    middle_rows = (rows_ref[p.t].astype(f32) + normed(total, post_gain)).astype(bf16)
    mid[...] = middle_rows
    mine[...] = normed(middle_rows.astype(f32), ff_gain).astype(bf16)
    lc = pltpu.make_async_copy(mine, xa.at[p.X, p.Y], loc.at[6])
    lc.start()
    last = []

    def view(dx, dy, h, sub):
        rows = slice(0, 32) if sub is None else ROW[sub]
        return xa.at[(p.X + 4 + dx) % 4, (p.Y + 4 + dy) % 4, rows, COL[h]]

    def middle_step():
        sib.extend(weight_take(p, cps, rest[0]))
        last.append(weight_send(p, cps, ws, True, 4))
        sib.extend(weight_take(p, cps, rest[1]))
        last.append(weight_send(p, cps, ws, False, 4))

    gather_grid(p, cps, lambda h: mine.at[:, COL[h]], view, 4, middle_step)
    sib += weight_take(p, cps, last[0])
    sib += weight_take(p, cps, last[1])
    for cp in px:
        cp.wait_recv()
    pages = pg[p.x, p.yb].astype(f32)
    for o in range(3):
        pages += rp[o].astype(f32)
    page_out[...] = pages.astype(bf16)
    for cp in sib:
        cp.wait_recv()
    for cp in locs[:3] + [lc]:
        cp.wait()
    cps.drain_sends()


def turned(v, cosine, sine, turn):
    c, s = cosine[...], sine[...]
    if turn is not None:
        c = jnp.where(turn, c, 1.0)
        s = jnp.where(turn, s, 0.0)
    a, b = v[:, :128], v[:, 128:]
    return jnp.concatenate([a * c - b * s, b * c + a * s], axis=1)


def feed_part(xin, mid, gain, wg, wu, wd, xa, send, recv, loc, vgu, vd, inner, y_ref, mine, *scratch):
    p = Place()
    def fetch(j):
        cols = pl.ds(pl.multiple_of(j * 128, 128), 128)
        return [pltpu.make_async_copy(w.at[:, cols], vgu.at[:, pl.ds(pl.multiple_of(j * 256 + k * 128, 128), 128)], loc.at[2 * j + k])
                for k, w in enumerate((wg, wu))]

    for j in range(5):
        for cp in fetch(j):
            cp.start()
    lw = pltpu.make_async_copy(wd, vd, loc.at[10])
    lw.start()
    barrier(p.around(4))
    cps = Copies(send, recv)

    def block(j, carry):
        for cp in fetch(j):
            cp.wait()
        x = xin[...].reshape(512, 2304)
        both = jnp.dot(x, vgu[:, pl.ds(pl.multiple_of(j * 256, 256), 256)], preferred_element_type=f32)
        gate, up = both[:, :128], both[:, 128:]
        made = jax.nn.gelu(gate, approximate=True) * up
        keep = jnp.zeros(made.shape, jnp.int32) + (j + 1 - p.x) > 0
        inner[:, pl.ds(pl.multiple_of(j * 128, 128), 128)] = jnp.where(keep, made, 0.0).astype(bf16)
        return carry

    lax.fori_loop(0, 5, block, 0)
    lw.wait()

    def lower(n, carry):
        w = vd[pl.ds(pl.multiple_of(n * 256, 256), 256), :]
        out = lax.dot_general(inner[...], w, (((1,), (1,)), ((), ())), preferred_element_type=f32)
        y_ref[:, :, :, pl.ds(pl.multiple_of(n * 256, 256), 256)] = out.astype(bf16).reshape(4, 4, 32, 256)
        return carry

    lax.fori_loop(0, 9, lower, 0)
    bufs, sums = reduce_bufs(scratch)
    total = jnp.concatenate(reduce_grid(p, cps, y_ref, bufs, sums, 4), axis=1)
    mine[...] = (mid[...].astype(f32) + normed(total, gain)).astype(bf16)
    lc = pltpu.make_async_copy(mine, xa.at[p.t], loc.at[11])
    lc.start()

    def view(dx, dy, h, sub):
        rows = slice(0, 32) if sub is None else ROW[sub]
        return xa.at[((p.X + 2 + dx) % 2) * 4 + (p.Y + 4 + dy) % 4, rows, COL[h]]

    gather_grid(p, cps, lambda h: mine.at[:, COL[h]], view, 2)
    lc.wait()
    cps.drain_sends()


def call(body, cid, ins, in_specs, outs, out_specs, n, n_loc=0, aliases=None, extra=()):
    scratch = [pltpu.SemaphoreType.DMA((n,)), pltpu.SemaphoreType.DMA((n,))]
    if n_loc:
        scratch.append(pltpu.SemaphoreType.DMA((n_loc,)))
    return pl.pallas_call(
        body,
        out_shape=[s if isinstance(s, jax.ShapeDtypeStruct) else jax.ShapeDtypeStruct(s, bf16) for s in outs],
        in_specs=in_specs,
        out_specs=out_specs,
        scratch_shapes=scratch + list(extra),
        input_output_aliases=aliases or {},
        compiler_params=pltpu.CompilerParams(collective_id=cid, has_side_effects=True),
        name=body.__name__,
    )(*ins)


def next_layer(fr, gain, wq, wk, cosine, sine, page, ho, q_ref, k_ref, page_out):
    p = Place()
    rows = fr[...].reshape(256, 2304).astype(f32)
    normal = normed(rows, gain).astype(bf16)
    q_ref[...] = turned(jnp.dot(normal, wq[...], preferred_element_type=f32), cosine, sine, None).astype(bf16)
    k_ref[...] = turned(jnp.dot(normal, wk[...], preferred_element_type=f32), cosine, sine, p.yb == 0).astype(bf16)
    begin = p.t * 288
    tile = pl.multiple_of((begin // 128) * 128, 128)
    window = fr[:, :, pl.ds(tile, 384)].reshape(256, 384).astype(f32)
    moved = jnp.transpose(pltpu.roll(window, (384 - begin % 128) % 384, 1))
    ho[...] = moved[:288, :].astype(bf16)
    page_out[...] = page[...]


def local_call(body, ins, in_specs, outs, scratch=()):
    return pl.pallas_call(
        body,
        out_shape=[jax.ShapeDtypeStruct(s, bf16) for s in outs],
        in_specs=in_specs,
        out_specs=[VM] * len(outs),
        scratch_shapes=list(scratch),
        name=body.__name__,
    )(*ins)


def quad_route(dx, dy):
    route = []
    for s in range(32):
        for t in range(8):
            route.append((s * 8 + t, ((s + 16 * dx) % 32) * 8 + (t ^ dy)))
    return route


def body(
    hidden, attn_gain, query_weight, kv_weight, out_weight, post_gain, ff_gain, ff_post_gain,
    gate_weight, up_weight, down_weight_t, next_gain, next_query_weight, next_kv_weight,
    lengths, pair_owner, page_table,
):
    wshape = (2, 16, 72, FFP)
    vmem = pltpu.VMEM
    angle = jax.ShapeDtypeStruct((256, 128), f32)
    mine = vmem((32, 2304), bf16)
    middle, xa, wg, wu, wd, page, cosine, sine = call(
        attention_part, 1,
        (lengths, pair_owner, page_table, hidden.T, gate_weight, up_weight, down_weight_t, jnp.asarray(FREQ), attn_gain,
         query_weight, kv_weight, out_weight, post_gain, ff_gain),
        [pl.BlockSpec(memory_space=pltpu.SMEM)] * 3 + [VM] * 11,
        [(32, 2304), (4, 4, 32, 2304), wshape, wshape, wshape, (2, 128, 256), angle, angle],
        [VM, VM, AN, AN, AN, VM, VM, VM], 224, 7, None,
        [vmem((8, 288, 256), bf16), vmem((8, 32, 2304), bf16), vmem((128, 256), bf16), vmem((128, 256), bf16),
         vmem((2, 128, 256), bf16), vmem((2, 8, 2, 128, 256), bf16), vmem((2, 2, 2, 128, 256), bf16),
         vmem((4, 256, 128), jnp.int32), vmem((4, 256, 256), f32), vmem((4, 256, 128), f32),
         vmem((2, 2, 2, 128, 256), bf16), vmem((2, 2, 2, 8, 128), f32), vmem((2, 2, 2, 128, 256), bf16),
         vmem((3, 2, 128, 256), bf16), vmem((3, 2, 8, 128), f32), vmem((3, 2, 128, 256), bf16),
         vmem((2, 4, 32, 2304), bf16), mine] + reduce_scratch(2),
    )
    (fr,) = call(
        feed_part, 2,
        (xa, middle, ff_post_gain, wg.reshape(2304, FFP), wu.reshape(2304, FFP), wd.reshape(2304, FFP)), [VM] * 3 + [AN] * 3,
        [(8, 32, 2304)], [VM], 60, 12, None,
        [vmem((2304, 2 * FFP), bf16), vmem((2304, FFP), bf16), vmem((512, FFP), bf16), vmem((4, 4, 32, 2304), bf16),
         mine] + reduce_scratch(4),
    )
    hidden_t, next_query, next_kv, kv_pages = local_call(
        next_layer, (fr, next_gain, next_query_weight, next_kv_weight, cosine, sine, page), [VM] * 7,
        [(288, 256), (256, 256), (256, 256), (2, 128, 256)],
    )
    return (hidden_t.T, next_query, next_kv, kv_pages)


def solution(mesh):
    wide = P("seq", "tensor")
    cols = P(None, "tensor")
    in_specs = (wide, P(), cols, cols, P("tensor", None), P(), P(), P(), wide, wide, wide, P(), cols, cols, P(), P(), P())
    out_specs = (wide, wide, wide, P("seq", None, "tensor"))
    return jax.shard_map(body, mesh=mesh, in_specs=in_specs, out_specs=out_specs, check_vma=False)
```

time: 209 us -> 160 us (0.77); the launches traced: 206 us -> 160 us
  Pallas kernels: 182 us -> 159 us
  local copies, waits for them, and re-layouts: 7.38 us -> 0 us
  starting transfers between devices: 4.99 us -> 0 us
  other arithmetic: 4.93 us -> 0 us
  between operations: 3.98 us -> 0.65 us
  matrix products: 2.64 us -> 0 us
    pallas_call x3 -> x1, Pallas kernels: 21.2 us -> 3.84 us  [local_call(): pl.pallas_call(body, out_shape=[jax.ShapeDtypeStruct(s, bf16) for s in ou...]
    pallas_call x1 -> x0, Pallas kernels: 9.09 us -> none  [body(): pl.pallas_call(attend, out_shape=[jax.ShapeDtypeStruct((4, 256, 256), bf1...]
    ppermute x3 -> x0, starting transfers between devices: 4.99 us -> none  [body(): lax.ppermute(page[o], ('seq', 'tensor'), quad_route(o // 2, o % 2))]
    pallas_call x5 -> x2, Pallas kernels: 152 us -> 156 us  [call(): pl.pallas_call(body, out_shape=[s if isinstance(s, jax.ShapeDtypeStruct)...]
    slice x3 -> x0, local copies, waits for them, and re-layouts: 2.79 us -> none  [the longest x2 1.43 us: body(): denominator = (den[0] + rd[0] + rd[1] + rd[2])[0][:, None]]
    dot_general x1 -> x0, matrix products: 2.64 us -> none  [body(): jnp.dot(attended, out_weight, preferred_element_type=f32).astype(bf16)]
    unnamed x6 -> x0, local copies, waits for them, and re-layouts: 2.61 us -> none
    convert_element_type x2 -> x0, other arithmetic: 2.28 us -> none  [the longest x1 1.63 us: body(): kv_pages = pages.astype(bf16).reshape(2, 128, 256)]
  transfers between devices with their start and end apart: 3 -> 0, of which waited for: 0 -> 0; matrix products, arithmetic and copies ran while one was open for 3% -> 0% of each run, Pallas kernels for 55% -> 0%
where the time goes in v4:
time: 160 us
  Pallas kernels  159 us (99%)
    pallas_call x2, Pallas kernels, call(): pl.pallas_call(body, out_shape=[s if isinstance(s, jax.ShapeDtypeStruct)...  156 us
    pallas_call x1, Pallas kernels, local_call(): pl.pallas_call(body, out_shape=[jax.ShapeDtypeStruct(s, bf16) for s in ou...  3.84 us

profile of v4, /device:TPU:4, one launch (start us, length us, event | category | flops | bytes accessed | tf_op | source)
XLA Modules:
  0.0 160.1 jit_solution(13650816933536899430)
XLA Ops:
  0.6 109.6 %attention_part.1 = (bf16[32,2304]{1,0:T(8,128)(2,1)}, bf16[4,4,32,2304]{3,2,1,0:T(8,128)(2,1)}, bf16[2,16,72,640]{3,2,1,0:T(8,128)(2,1)}, bf16[2,16,72,640]{3,2...) custom-call(s32[4]{0:T(128)} %lengths.1, ...), custom_call_target="tpu_custom_call" | custom-call | tf_op jit(solution)/shard_map/attention_part/pallas_call | solution.py:577
  110.3 45.9 %feed_part.1.fr = bf16[8,32,2304]{2,1,0:T(8,128)(2,1)} custom-call(bf16[4,4,32,2304]{3,2,1,0:T(8,128)(2,1)} %get-tuple-element.16.xin, bf16[32,2304]{1,0:T(8,128)(2,1)} %get-tuple-element.17.mid, f32[2304]{0:T(1024)} %gain.2, bf16[2304,640]{1,0:T(8,128)(2,1)} %bitcast.5, bf16[2304,640]{1,0:T(8,128)(2,1)} %bitcast.6, bf16[2304,640]{1,0:T(8,128)(2,1)} %bitcast.7), custom_call_target="tpu_custom_call" | custom-call | tf_op jit(solution)/shard_map/feed_part/pallas_call | solution.py:577
  156.2 3.8 %next_layer.1 = (bf16[288,256]{1,0:T(8,128)(2,1)}, bf16[256,256]{1,0:T(8,128)(2,1)}, bf16[256,256]{1,0:T(8,128)(2,1)}, bf16[2,128,256]{2,1,0:T(8,128)(2,1)}) custom-call(bf16[8,32,2304]{2,1,0:T(8,128)(2,1)} %feed_part.1.fr, f32[2304]{0:T(1024)} %gain.3, bf16[2304,256]{1,0:T(8,128)(2,1)} %wq.3, bf16[2304,256]{1,0:T(8,128)(2,1)} %wk.3, ...), custom_call_target="tpu_custom_call" | custom-call | tf_op jit(solution)/shard_map/next_layer/pallas_call | solution.py:604

commit v5 on v4

--- a/solution.py
+++ b/solution.py
@@ -249,14 +249,18 @@
     return values * lax.rsqrt(jnp.mean(values * values, axis=1, keepdims=True) + EPS) * gain[...][None, :]
 
 
+def strip(org, slot):
+    return pl.ds(pl.multiple_of((org * 16 + slot) * 72, 8), 72)
+
+
 def weight_send(p, cps, ws, own, d):
     org = p.x if own else 1 - p.x
     got = []
     for sign, dev in ((-1, p.zp()), (1, p.zm())):
         if d == 4 and (sign == -1) != own:
             continue
-        slot = ((p.z + 8 + sign * (d - 1)) % 8) * 2 + p.c
-        got += [(cps.go(w.at[org, slot], w.at[org, slot], dev), w, sign) for w in ws]
+        here = strip(org, ((p.z + 8 + sign * (d - 1)) % 8) * 2 + p.c)
+        got += [(cps.go(w.at[here], w.at[here], dev), w, sign) for w in ws]
     return org, got, d
 
 
@@ -265,8 +269,8 @@
     out = []
     for cp, w, sign in got:
         cp.wait_recv()
-        slot = ((p.z + 8 + sign * d) % 8) * 2 + p.c
-        out.append(cps.go(w.at[org, slot], w.at[org, slot], p.sib()))
+        here = w.at[strip(org, ((p.z + 8 + sign * d) % 8) * 2 + p.c)]
+        out.append(cps.go(here, here, p.sib()))
     return out
 
 
@@ -277,11 +281,11 @@
     return jnp.where(tags >= e2, e2, jnp.where(tags >= e1, e1, jnp.where(tags >= e0, e0, 0)))
 
 
-def attention_part(
-    lengths, owner, table, ht, gate, up, down, freq, attn_gain, wq, wk, wo, post_gain, ff_gain,
-    mid, xa, wg, wu, wd, page_out, cosine, sine,
+def whole_layer(
+    lengths, owner, table, ht, gate, up, down, freq, attn_gain, wq, wk, wo, post_gain, ff_gain, last_gain,
+    fr, wg, wu, wd, page_out, cosine, sine,
     send, recv, loc, xt, rows_ref, stay, go, q_ref, kv, qa, start_ref, acc, den, num, dn, pg, rn, rd, rp, part, mine,
-    *scratch,
+    mid, xa, vg, vu, vd, inner, y_ref, final, *scratch,
 ):
     p = Place()
     quads = [p.quad(o) for o in range(1, 4)]
@@ -289,16 +293,18 @@
     cps = Copies(send, recv)
     ws = (wg, wu, wd)
     slot = p.z * 2 + p.c
+    near_rows = strip(p.x, slot)
+    far_rows = strip(1 - p.x, slot)
 
     columns = pl.ds(pl.multiple_of(p.x * FFO, 128), FFP)
     other = pl.ds(pl.multiple_of((1 - p.x) * FFO, 128), FFP)
-    swaps = [cps.go(a.at[:, other], w.at[p.x, slot], p.xpart()) for a, w in zip((gate, up, down), ws)]
-    ring = [(cps.go(a.at[:, columns], w.at[p.x, slot], dev), w, sign)
+    swaps = [cps.go(a.at[:, other], w.at[near_rows], p.xpart()) for a, w in zip((gate, up, down), ws)]
+    ring = [(cps.go(a.at[:, columns], w.at[near_rows], dev), w, sign)
             for sign, dev in ((-1, p.zp()), (1, p.zm())) for a, w in zip((gate, up, down), ws)]
-    locs = [pltpu.make_async_copy(a.at[:, columns], w.at[p.x, slot], loc.at[i])
+    locs = [pltpu.make_async_copy(a.at[:, columns], w.at[near_rows], loc.at[i])
             for i, (a, w) in enumerate(zip((gate, up, down), ws))]
     locs.append(pltpu.make_async_copy(ht, xt.at[p.t], loc.at[3]))
-    sib = [cps.go(a.at[:, columns], w.at[p.x, slot], p.sib()) for a, w in zip((gate, up, down), ws)]
+    sib = [cps.go(a.at[:, columns], w.at[near_rows], p.sib()) for a, w in zip((gate, up, down), ws)]
     for cp in locs:
         cp.start()
 
@@ -334,7 +340,7 @@
             cp.wait_recv()
         swapped.append(weight_send(p, cps, ws, False, 1))
         for w in ws:
-            sib.append(cps.go(w.at[1 - p.x, slot], w.at[1 - p.x, slot], p.sib()))
+            sib.append(cps.go(w.at[far_rows], w.at[far_rows], p.sib()))
 
     gather_grid(p, cps, lambda h: ht.at[pl.ds(h * 144, 144)], view_hidden, 2, middle)
     locs[3].wait()
@@ -457,7 +463,6 @@
         return carry
 
     lax.fori_loop(0, 4, choose, 0)
-    px = [cps.go(pg.at[x, yb], rp.at[o], d) for o, (x, yb, d) in enumerate(quads)]
     for cp in ex:
         cp.wait_recv()
     total = num[p.x, p.yb].astype(f32)
@@ -475,7 +480,7 @@
     sib += weight_take(p, cps, rest[1])
     rest = [weight_send(p, cps, ws, True, 3), weight_send(p, cps, ws, False, 3)]
 
-    bufs, sums = reduce_bufs(scratch)
+    bufs, sums = reduce_bufs(scratch[:26])
     total = jnp.concatenate(reduce_grid(p, cps, part, bufs, sums, 2), axis=1)
     middle_rows = (rows_ref[p.t].astype(f32) + normed(total, post_gain)).astype(bf16)
     mid[...] = middle_rows
@@ -497,16 +502,54 @@
     gather_grid(p, cps, lambda h: mine.at[:, COL[h]], view, 4, middle_step)
     sib += weight_take(p, cps, last[0])
     sib += weight_take(p, cps, last[1])
+    for cp in sib:
+        cp.wait_recv()
+    for cp in locs[:3] + [lc]:
+        cp.wait()
+    loads = [pltpu.make_async_copy(w, v, loc.at[7 + i]) for i, (w, v) in enumerate(((wg, vg), (wu, vu), (wd, vd)))]
+    for cp in loads:
+        cp.start()
+    px = [cps.go(pg.at[x, yb], rp.at[o], d) for o, (x, yb, d) in enumerate(quads)]
+    loads[0].wait()
+    loads[1].wait()
+
+    def block(j, carry):
+        cols = pl.ds(pl.multiple_of(j * 128, 128), 128)
+        pair_cols = jnp.concatenate([vg[:, cols], vu[:, cols]], axis=1)
+        both = jnp.dot(xa[...].reshape(512, 2304), pair_cols, preferred_element_type=f32)
+        made = jax.nn.gelu(both[:, :128], approximate=True) * both[:, 128:]
+        keep = jnp.zeros(made.shape, jnp.int32) + (j + 1 - p.x) > 0
+        inner[:, cols] = jnp.where(keep, made, 0.0).astype(bf16)
+        return carry
+
+    lax.fori_loop(0, 5, block, 0)
+    loads[2].wait()
+
+    def lower(n, carry):
+        w = vd[pl.ds(pl.multiple_of(n * 256, 256), 256), :]
+        out = lax.dot_general(inner[...], w, (((1,), (1,)), ((), ())), preferred_element_type=f32)
+        y_ref[:, :, :, pl.ds(pl.multiple_of(n * 256, 256), 256)] = out.astype(bf16).reshape(4, 4, 32, 256)
+        return carry
+
+    lax.fori_loop(0, 9, lower, 0)
+    bufs, sums = reduce_bufs(scratch[26:])
+    total = jnp.concatenate(reduce_grid(p, cps, y_ref, bufs, sums, 4), axis=1)
+    final[...] = (mid[...].astype(f32) + normed(total, last_gain)).astype(bf16)
+    lc = pltpu.make_async_copy(final, fr.at[p.t], loc.at[10])
+    lc.start()
+
+    def view_final(dx, dy, h, sub):
+        rows = slice(0, 32) if sub is None else ROW[sub]
+        return fr.at[((p.X + 2 + dx) % 2) * 4 + (p.Y + 4 + dy) % 4, rows, COL[h]]
+
+    gather_grid(p, cps, lambda h: final.at[:, COL[h]], view_final, 2)
     for cp in px:
         cp.wait_recv()
     pages = pg[p.x, p.yb].astype(f32)
     for o in range(3):
         pages += rp[o].astype(f32)
     page_out[...] = pages.astype(bf16)
-    for cp in sib:
-        cp.wait_recv()
-    for cp in locs[:3] + [lc]:
-        cp.wait()
+    lc.wait()
     cps.drain_sends()
 
 
@@ -517,57 +560,6 @@
         s = jnp.where(turn, s, 0.0)
     a, b = v[:, :128], v[:, 128:]
     return jnp.concatenate([a * c - b * s, b * c + a * s], axis=1)
-
-
-def feed_part(xin, mid, gain, wg, wu, wd, xa, send, recv, loc, vgu, vd, inner, y_ref, mine, *scratch):
-    p = Place()
-    def fetch(j):
-        cols = pl.ds(pl.multiple_of(j * 128, 128), 128)
-        return [pltpu.make_async_copy(w.at[:, cols], vgu.at[:, pl.ds(pl.multiple_of(j * 256 + k * 128, 128), 128)], loc.at[2 * j + k])
-                for k, w in enumerate((wg, wu))]
-
-    for j in range(5):
-        for cp in fetch(j):
-            cp.start()
-    lw = pltpu.make_async_copy(wd, vd, loc.at[10])
-    lw.start()
-    barrier(p.around(4))
-    cps = Copies(send, recv)
-
-    def block(j, carry):
-        for cp in fetch(j):
-            cp.wait()
-        x = xin[...].reshape(512, 2304)
-        both = jnp.dot(x, vgu[:, pl.ds(pl.multiple_of(j * 256, 256), 256)], preferred_element_type=f32)
-        gate, up = both[:, :128], both[:, 128:]
-        made = jax.nn.gelu(gate, approximate=True) * up
-        keep = jnp.zeros(made.shape, jnp.int32) + (j + 1 - p.x) > 0
-        inner[:, pl.ds(pl.multiple_of(j * 128, 128), 128)] = jnp.where(keep, made, 0.0).astype(bf16)
-        return carry
-
-    lax.fori_loop(0, 5, block, 0)
-    lw.wait()
-
-    def lower(n, carry):
-        w = vd[pl.ds(pl.multiple_of(n * 256, 256), 256), :]
-        out = lax.dot_general(inner[...], w, (((1,), (1,)), ((), ())), preferred_element_type=f32)
-        y_ref[:, :, :, pl.ds(pl.multiple_of(n * 256, 256), 256)] = out.astype(bf16).reshape(4, 4, 32, 256)
-        return carry
-
-    lax.fori_loop(0, 9, lower, 0)
-    bufs, sums = reduce_bufs(scratch)
-    total = jnp.concatenate(reduce_grid(p, cps, y_ref, bufs, sums, 4), axis=1)
-    mine[...] = (mid[...].astype(f32) + normed(total, gain)).astype(bf16)
-    lc = pltpu.make_async_copy(mine, xa.at[p.t], loc.at[11])
-    lc.start()
-
-    def view(dx, dy, h, sub):
-        rows = slice(0, 32) if sub is None else ROW[sub]
-        return xa.at[((p.X + 2 + dx) % 2) * 4 + (p.Y + 4 + dy) % 4, rows, COL[h]]
-
-    gather_grid(p, cps, lambda h: mine.at[:, COL[h]], view, 2)
-    lc.wait()
-    cps.drain_sends()
 
 
 def call(body, cid, ins, in_specs, outs, out_specs, n, n_loc=0, aliases=None, extra=()):
@@ -624,30 +616,25 @@
     gate_weight, up_weight, down_weight_t, next_gain, next_query_weight, next_kv_weight,
     lengths, pair_owner, page_table,
 ):
-    wshape = (2, 16, 72, FFP)
+    wshape = (2304, FFP)
     vmem = pltpu.VMEM
     angle = jax.ShapeDtypeStruct((256, 128), f32)
     mine = vmem((32, 2304), bf16)
-    middle, xa, wg, wu, wd, page, cosine, sine = call(
-        attention_part, 1,
+    fr, wg, wu, wd, page, cosine, sine = call(
+        whole_layer, 1,
         (lengths, pair_owner, page_table, hidden.T, gate_weight, up_weight, down_weight_t, jnp.asarray(FREQ), attn_gain,
-         query_weight, kv_weight, out_weight, post_gain, ff_gain),
-        [pl.BlockSpec(memory_space=pltpu.SMEM)] * 3 + [VM] * 11,
-        [(32, 2304), (4, 4, 32, 2304), wshape, wshape, wshape, (2, 128, 256), angle, angle],
-        [VM, VM, AN, AN, AN, VM, VM, VM], 224, 7, None,
+         query_weight, kv_weight, out_weight, post_gain, ff_gain, ff_post_gain),
+        [pl.BlockSpec(memory_space=pltpu.SMEM)] * 3 + [VM] * 12,
+        [(8, 32, 2304), wshape, wshape, wshape, (2, 128, 256), angle, angle],
+        [VM, AN, AN, AN, VM, VM, VM], 280, 11, None,
         [vmem((8, 288, 256), bf16), vmem((8, 32, 2304), bf16), vmem((128, 256), bf16), vmem((128, 256), bf16),
          vmem((2, 128, 256), bf16), vmem((2, 8, 2, 128, 256), bf16), vmem((2, 2, 2, 128, 256), bf16),
          vmem((4, 256, 128), jnp.int32), vmem((4, 256, 256), f32), vmem((4, 256, 128), f32),
          vmem((2, 2, 2, 128, 256), bf16), vmem((2, 2, 2, 8, 128), f32), vmem((2, 2, 2, 128, 256), bf16),
          vmem((3, 2, 128, 256), bf16), vmem((3, 2, 8, 128), f32), vmem((3, 2, 128, 256), bf16),
-         vmem((2, 4, 32, 2304), bf16), mine] + reduce_scratch(2),
-    )
-    (fr,) = call(
-        feed_part, 2,
-        (xa, middle, ff_post_gain, wg.reshape(2304, FFP), wu.reshape(2304, FFP), wd.reshape(2304, FFP)), [VM] * 3 + [AN] * 3,
-        [(8, 32, 2304)], [VM], 60, 12, None,
-        [vmem((2304, 2 * FFP), bf16), vmem((2304, FFP), bf16), vmem((512, FFP), bf16), vmem((4, 4, 32, 2304), bf16),
-         mine] + reduce_scratch(4),
+         vmem((2, 4, 32, 2304), bf16), mine, mine, vmem((4, 4, 32, 2304), bf16), vmem((2304, FFP), bf16),
+         vmem((2304, FFP), bf16), vmem((2304, FFP), bf16), vmem((512, FFP), bf16), vmem((4, 4, 32, 2304), bf16), mine]
+        + reduce_scratch(2) + reduce_scratch(4),
     )
     hidden_t, next_query, next_kv, kv_pages = local_call(
         next_layer, (fr, next_gain, next_query_weight, next_kv_weight, cosine, sine, page), [VM] * 7,

time: 160 us -> 152 us (0.950)
  Pallas kernels: 159 us -> 151 us
    pallas_call x2 -> x1, Pallas kernels: 156 us -> 147 us  [call(): pl.pallas_call(body, out_shape=[s if isinstance(s, jax.ShapeDtypeStruct)...]
where the time goes in v5:
time: 152 us
  Pallas kernels  151 us (99%)
    pallas_call x1, Pallas kernels, call(): pl.pallas_call(body, out_shape=[s if isinstance(s, jax.ShapeDtypeStruct)...  147 us
    pallas_call x1, Pallas kernels, local_call(): pl.pallas_call(body, out_shape=[jax.ShapeDtypeStruct(s, bf16) for s in ou...  3.84 us

profile of v5, /device:TPU:4, one launch (start us, length us, event | category | flops | bytes accessed | tf_op | source)
XLA Modules:
  0.0 151.5 jit_solution(884184970143920364)
XLA Ops:
  0.6 147.1 %whole_layer.1 = (bf16[8,32,2304]{2,1,0:T(8,128)(2,1)}, bf16[2304,640]{1,0:T(8,128)(2,1)}, bf16[2304,640]{1,0:T(8,128)(2,1)}, bf16[2304,640]{1,0:T(8,128)(2,1)},...) custom-call(s32[4]{0:T(128)} %lengths.1, s32[32]{0:T(128)} %owner.1, s32[64]{0:T(128)} %table.1, ...), custom_call_target="tpu_custom_call" | custom-call | tf_op jit(solution)/shard_map/whole_layer/pallas_call | solution.py:569
  147.7 3.8 %next_layer.1 = (bf16[288,256]{1,0:T(8,128)(2,1)}, bf16[256,256]{1,0:T(8,128)(2,1)}, bf16[256,256]{1,0:T(8,128)(2,1)}, bf16[2,128,256]{2,1,0:T(8,128)(2,1)}) custom-call(bf16[8,32,2304]{2,1,0:T(8,128)(2,1)} %get-tuple-element.12.fr, f32[2304]{0:T(1024)} %gain.1, bf16[2304,256]{1,0:T(8,128)(2,1)} %wq.3, bf16[2304,256]{1,0:T(8,128)(2,1)} %wk.3, ...), custom_call_target="tpu_custom_call" | custom-call | tf_op jit(solution)/shard_map/next_layer/pallas_call | solution.py:596
